TPU v7x, 256 devices: a whole 4x4x8 slice. The times are simulated.
256 devices in a mesh: gx: 8 (over x, core), gy: 4 (over y), gz: 8 (over z).
Axes of the slice: x: 4, y: 4, z: 8, core: 2. Of those that a mesh axis runs over, the one named last changes fastest.
Arguments:
- right_side: float32 [192, 128, 1024], P('gx', 'gy', 'gz'), may hold values from -6 to 6
- conductance: float32 [192, 128, 1024], P('gx', 'gy', 'gz'), may hold values from 0.05 to 10
- absorption: float32 [192, 128, 1024], P('gx', 'gy', 'gz'), may hold values from 0.002 to 0.02
- block_agg: int32 [96, 64, 512], P('gx', 'gy', 'gz'), may hold values from 0 to 127, as said below
Outputs:
- solution: float32 [192, 128, 1024], P('gx', 'gy', 'gz')
Inputs may be any that keep to these rules, and one draw needn't show every extreme that they name: `block_agg`: aggregates never leave their brick; in every brick each number 0 to 127 names at least one block.
All inputs are finite; a program needn't handle non-finite values.
Results may differ from a plain program's by a relative error of at most 0.0003.
Values sent between devices are 32-bit elements; how exact they have to be, the bound alone decides.
A program may use at most 128 MiB of HBM per device.

v0:
```python
import jax
import jax.numpy as jnp
from jax import lax
from jax.experimental import pallas as pl
from jax.experimental.pallas import tpu as pltpu
from jax.sharding import PartitionSpec as P

AGG = 128
POST = 4
KC = 8
OMEGA_FINE = 0.8
OMEGA_COARSE = 0.7
CX, CY, CZ = 24, 32, 128
BX = CX // 2
TOP = 8
END = TOP + CY
AXES = ("gx", "gy", "gz")
F32 = jnp.float32
BF16 = jnp.bfloat16
NT = (((1,), (1,)), ((), ()))


def harmonic(one_side, other_side):
    summed = one_side + other_side
    return 2.0 * (one_side * other_side) / summed


def safe_harmonic(one_side, other_side):
    summed = one_side + other_side
    return 2.0 * (one_side * other_side) / jnp.where(summed > 0.0, summed, 1.0)


def lanes_of(shape):
    return lax.broadcasted_iota(jnp.int32, shape, 1)


def rows_of(shape):
    return lax.broadcasted_iota(jnp.int32, shape, 0)


def lane_roll(values, shift):
    return pltpu.roll(values, shift % CZ if isinstance(shift, int) else shift, 1)


def row_roll(values, shift):
    return pltpu.roll(values, shift % values.shape[0], 0)


def pack(low, high, plane, x):
    lane = lanes_of((8, CZ))
    for g in range(4):
        k = 4 * x + g
        piece = plane[8 * g : 8 * g + 8]
        low = jnp.where(lane == k, lane_roll(piece, k), low)
        high = jnp.where(lane == k, lane_roll(piece, k + 1), high)
    return low, high


def unpack_low(packed, x):
    return jnp.concatenate([lane_roll(packed, lax.rem(CZ - (4 * x + g), CZ)) for g in range(4)], axis=0)


def unpack_high(packed, x):
    return jnp.concatenate([lane_roll(packed, CZ - 1 - (4 * x + g)) for g in range(4)], axis=0)


def quad_sum(values):
    pair = values + row_roll(values, -1)
    return pair + lane_roll(pair, -1)


def squeeze_cells(values):
    even = (lanes_of(values.shape) & 1) == 0
    return jnp.where(even, values, lane_roll(row_roll(values, -2), 1))


def split(values):
    high = values.astype(BF16).astype(F32)
    return high, values - high


def spread_row(row):
    return jnp.broadcast_to(row, (16, CZ)).astype(BF16)


def kernel(
    b_hbm, k_hbm, a_hbm, l_hbm, out_hbm,
    bv, av, kp, lv, v, gw, c0, dg, lc, el, ew,
    kzs, kzh, lxh, lys, lyh, lzs, lzh, zs, zh,
    wxf, wyf, fzf, xs, ys, acc, mf, mm, cs, ch,
    local_sem, send_sem, recv_sem,
):
    pos = [lax.axis_index(a) for a in AXES]
    size = [lax.axis_size(a) for a in AXES]
    has = []
    dev = []
    for axis in range(3):
        has.append(pos[axis] > 0)
        dev.append({AXES[axis]: pos[axis] - 1})
        has.append(pos[axis] < size[axis] - 1)
        dev.append({AXES[axis]: pos[axis] + 1})

    def exchange_of(kind, slot):
        if kind == "k":
            src = [kp.at[1, TOP:END], kp.at[CX, TOP:END], kp.at[1 : CX + 1, TOP : TOP + 1],
                   kp.at[1 : CX + 1, END - 1 : END], kzs.at[0], kzs.at[1]]
            dst = [kp.at[0, TOP:END], kp.at[CX + 1, TOP:END], kp.at[1 : CX + 1, TOP - 1 : TOP],
                   kp.at[1 : CX + 1, END : END + 1], kzh.at[0], kzh.at[1]]
            sem = 0
        elif kind == "l":
            src = [lc.at[0, TOP:END], lc.at[BX - 1, TOP:END], lys.at[0], lys.at[1], lzs.at[0], lzs.at[1]]
            dst = [lxh.at[0], lxh.at[1], lyh.at[0], lyh.at[1], lzh.at[0], lzh.at[1]]
            sem = 1
        elif kind == "v":
            src = [v.at[slot, 1, TOP:END], v.at[slot, CX, TOP:END], v.at[slot, 1 : CX + 1, TOP : TOP + 1],
                   v.at[slot, 1 : CX + 1, END - 1 : END], zs.at[slot, 0], zs.at[slot, 1]]
            dst = [v.at[slot, 0, TOP:END], v.at[slot, CX + 1, TOP:END], v.at[slot, 1 : CX + 1, TOP - 1 : TOP],
                   v.at[slot, 1 : CX + 1, END : END + 1], zh.at[slot, 0], zh.at[slot, 1]]
            sem = 2 + slot
        else:
            src = [cs.at[slot]] * 6
            dst = [ch.at[slot, d] for d in range(6)]
            sem = 4 + slot
        return src, dst, sem

    def copy_to(kind, slot, d):
        src, dst, sem = exchange_of(kind, slot)
        return pltpu.make_async_remote_copy(
            src[d], dst[d ^ 1], send_sem.at[sem, d], recv_sem.at[sem, d ^ 1],
            device_id=dev[d], device_id_type=pl.DeviceIdType.MESH)

    def copy_from(kind, slot, d):
        src, dst, sem = exchange_of(kind, slot)
        return pltpu.make_async_remote_copy(
            src[d], dst[d], send_sem.at[sem, d], recv_sem.at[sem, d],
            device_id=dev[d], device_id_type=pl.DeviceIdType.MESH)

    def start(kind, slot=0, sides=range(6)):
        for d in sides:
            @pl.when(has[d])
            def _():
                copy_to(kind, slot, d).start()

    def finish(kind, slot=0):
        for d in range(6):
            @pl.when(has[d])
            def _():
                copy_from(kind, slot, d).wait_recv()
        for d in range(6):
            @pl.when(has[d])
            def _():
                copy_to(kind, slot, d).wait_send()

    load_k = pltpu.make_async_copy(k_hbm, kp.at[1 : CX + 1, TOP:END], local_sem.at[0])
    load_l = pltpu.make_async_copy(l_hbm, lv, local_sem.at[1])
    load_a = pltpu.make_async_copy(a_hbm, av, local_sem.at[2])
    load_b = pltpu.make_async_copy(b_hbm, bv, local_sem.at[3])
    load_k.start()
    load_l.start()
    load_a.start()
    load_b.start()

    zero_plane = jnp.zeros((CY, CZ), F32)
    zero_tile = jnp.zeros((8, CZ), F32)
    for edge in (0, CX + 1):
        kp[edge, TOP:END] = zero_plane
        v[0, edge, TOP:END] = zero_plane
        v[1, edge, TOP:END] = zero_plane
    for side in range(2):
        lxh[side] = zero_plane
        lyh[side] = jnp.zeros((16, CZ), F32)
        lys[side] = jnp.zeros((16, CZ), F32)
        wyf[side] = jnp.zeros((16, CZ), F32)
        kzh[side] = zero_tile
        lzh[side] = zero_tile
        for slot in range(2):
            zh[slot, side] = zero_tile
    for slot in range(2):
        for d in range(6):
            ch[slot, d] = zero_tile

    def clear_rows(x, carry):
        for edge in (TOP - 8, END):
            kp[x + 1, edge : edge + 8] = zero_tile
            v[0, x + 1, edge : edge + 8] = zero_tile
            v[1, x + 1, edge : edge + 8] = zero_tile
        return carry

    lax.fori_loop(0, CX, clear_rows, 0)

    barrier = pltpu.get_barrier_semaphore()
    count = jnp.int32(0)
    for d in range(6):
        @pl.when(has[d])
        def _():
            pl.semaphore_signal(barrier, inc=1, device_id=dev[d], device_id_type=pl.DeviceIdType.MESH)
        count = count + has[d].astype(jnp.int32)
    pl.semaphore_wait(barrier, count)

    load_k.wait()
    start("k", 0, range(4))

    def pack_k(x, carry):
        return pack(*carry, kp[x + 1, TOP:END], x)

    kz_low, kz_high = lax.fori_loop(0, CX, pack_k, (zero_tile, zero_tile))
    kzs[0] = kz_low
    kzs[1] = kz_high
    start("k", 0, (4, 5))

    load_l.wait()
    labels = lv[...].reshape(BX * 16, 64).astype(F32).astype(BF16)
    widen = jnp.where(lanes_of((64, CZ)) // 2 == rows_of((64, CZ)), 1.0, 0.0).astype(BF16)
    wide = jnp.dot(labels, widen, preferred_element_type=F32).astype(BF16)
    tall_shape = (BX * CY, BX * 16)
    heighten = jnp.where(rows_of(tall_shape) // 2 == lanes_of(tall_shape), 1.0, 0.0).astype(BF16)
    cells = jnp.dot(heighten, wide, preferred_element_type=F32)
    for x in range(BX):
        lc[x, TOP:END] = cells[x * CY : (x + 1) * CY]
        lc[x, END : END + 8] = zero_tile
        lys[0, x : x + 1] = cells[x * CY : x * CY + 1]
        lys[1, x : x + 1] = cells[x * CY + CY - 1 : x * CY + CY]

    def pack_l(block, carry):
        plane = lc[block, TOP:END]
        return pack(*pack(*carry, plane, 2 * block), plane, 2 * block + 1)

    lz_low, lz_high = lax.fori_loop(0, BX, pack_l, (zero_tile, zero_tile))
    lzs[0] = lz_low
    lzs[1] = lz_high
    start("l")

    load_a.wait()
    load_b.wait()
    finish("k")

    lane = lanes_of((CY, CZ))
    row = rows_of((CY, CZ))
    fzf[0] = safe_harmonic(kzs[0], kzh[0])
    fzf[1] = safe_harmonic(kzs[1], kzh[1])

    def coefficients(x, fx_low):
        centre = kp[x + 1, TOP:END]
        fx_high = harmonic(centre, kp[x + 2, TOP:END])
        fy_low = harmonic(kp[x + 1, TOP - 1 : END - 1], centre)
        last = harmonic(centre[CY - 8 :], kp[x + 1, END - 7 : END + 1])
        last = jnp.concatenate([last] * 4, axis=0)
        fy_high = jnp.where(row == CY - 1, last, row_roll(fy_low, -1))
        fz_low = harmonic(lane_roll(centre, 1), centre)
        fz_low = jnp.where(lane == 0, unpack_low(fzf[0], x), fz_low)
        fz_high = jnp.where(lane == CZ - 1, unpack_high(fzf[1], x), lane_roll(fz_low, -1))
        diag = av[x] + fx_low + fx_high + fy_low + fy_high + fz_low + fz_high
        scale = OMEGA_FINE / diag
        for n, face in enumerate((fx_low, fx_high, fy_low, fy_high, fz_low, fz_high)):
            gw[n, x] = scale * face
        first = scale * bv[x]
        c0[x] = first
        dg[x] = diag
        v[0, x + 1, TOP:END] = first
        return first, fx_high, fy_low, fy_high, fz_high

    def block_step(block, carry):
        fx_low, low, high = carry
        x = 2 * block
        first_0, fx_mid, fy_low_0, fy_high_0, fz_high_0 = coefficients(x, fx_low)
        low, high = pack(low, high, first_0, x)
        first_1, fx_high, fy_low_1, fy_high_1, fz_high_1 = coefficients(x + 1, fx_mid)
        low, high = pack(low, high, first_1, x + 1)
        wx = quad_sum(fx_high)
        wy = fy_high_0 + fy_high_1
        wy = row_roll(wy + lane_roll(wy, -1), -1)
        wz = fz_high_0 + fz_high_1
        wz = lane_roll(wz + row_roll(wz, -1), -1)
        wa = 0.5 * quad_sum(av[x] + av[x + 1])
        wy_low = (fy_low_0 + fy_low_1)[0:1]
        wyf[0, pl.ds(block, 1)] = wy_low + lane_roll(wy_low, -1)
        wyf[1, pl.ds(block, 1)] = wy[CY - 2 : CY - 1]
        own = lc[block, TOP:END]
        lx = lc[jnp.minimum(block + 1, BX - 1), TOP:END]
        ly = lc[block, TOP + 2 : END + 2]
        lz = lane_roll(own, -2)
        lx = jnp.where(lx == own, -1.0, lx)
        ly = jnp.where((ly == own) | (row >= CY - 2), -1.0, ly)
        lz = jnp.where((lz == own) | (lane >= CZ - 2), -1.0, lz)
        same = ly == lx
        wx = wx + jnp.where(same, wy, 0.0)
        ly = jnp.where(same, -1.0, ly)
        same = lz == lx
        wx = wx + jnp.where(same, wz, 0.0)
        lz = jnp.where(same, -1.0, lz)
        same = lz == ly
        wy = wy + jnp.where(same, wz, 0.0)
        lz = jnp.where(same, -1.0, lz)
        for n, field in enumerate((own, lx, ly, lz)):
            el[n, block] = squeeze_cells(field)
        for n, field in enumerate((wa, wx, wy, wz)):
            ew[n, block] = squeeze_cells(field)
        return fx_high, low, high

    fx_first = harmonic(kp[0, TOP:END], kp[1, TOP:END])
    wxf[0] = quad_sum(fx_first)
    fx_last, z_low, z_high = lax.fori_loop(0, BX, block_step, (fx_first, zero_tile, zero_tile))
    wxf[1] = quad_sum(fx_last)
    zs[0, 0] = z_low
    zs[0, 1] = z_high
    start("v", 0)

    number = rows_of((16, CZ)).astype(F32)
    numbers = [(number + 16.0 * q).astype(BF16) for q in range(8)]
    one = jnp.ones((16, CZ), BF16)
    zero = jnp.zeros((16, CZ), BF16)

    def place(at, lhs_label, pairs):
        lhs_label = spread_row(lhs_label)
        spread = []
        for label, weight in pairs:
            high, low = split(weight)
            spread.append((spread_row(label), spread_row(high), spread_row(low)))
        for q in range(8):
            xs[16 * q : 16 * q + 16, at : at + CZ] = jnp.where(lhs_label == numbers[q], one, zero)
            y_high = zero
            y_low = zero
            for label, high, low in spread:
                hit = label == numbers[q]
                y_high = jnp.where(hit, high, y_high)
                y_low = jnp.where(hit, low, y_low)
            ys[16 * q : 16 * q + 16, at : at + CZ] = y_high
            ys[AGG + 16 * q : AGG + 16 * q + 16, at : at + CZ] = y_low

    acc[...] = jnp.zeros((AGG, 2 * AGG), F32)

    def own_step(block, carry):
        for m in range(8):
            rows = slice(4 * m, 4 * m + 1)
            pairs = [(el[n, block, rows], ew[n, block, rows]) for n in range(4)]
            place(m * CZ, pairs[0][0], pairs)
        acc[...] += lax.dot_general(xs[...], ys[...], NT, preferred_element_type=F32)
        return carry

    lax.fori_loop(0, BX, own_step, 0)
    half = acc[:, :AGG] + acc[:, AGG:]
    mf[0:AGG] = half + half.T

    def neighbours(slot, x):
        centre = v[slot, x + 1, TOP:END]
        z_low = jnp.where(lane == 0, unpack_low(zh[slot, 0], x), lane_roll(centre, 1))
        z_high = jnp.where(lane == CZ - 1, unpack_high(zh[slot, 1], x), lane_roll(centre, -1))
        total = c0[x]
        total = total + gw[0, x] * v[slot, x, TOP:END] + gw[1, x] * v[slot, x + 2, TOP:END]
        total = total + gw[2, x] * v[slot, x + 1, TOP - 1 : END - 1]
        total = total + gw[3, x] * v[slot, x + 1, TOP + 1 : END + 1]
        total = total + gw[4, x] * z_low + gw[5, x] * z_high
        return centre, total

    def sweep(slot, other):
        def step(x, carry):
            centre, total = neighbours(slot, x)
            new = total + (1.0 - OMEGA_FINE) * centre
            v[other, x + 1, TOP:END] = new
            return pack(*carry, new, x)

        low, high = lax.fori_loop(0, CX, step, (zero_tile, zero_tile))
        zs[other, 0] = low
        zs[other, 1] = high

    finish("v", 0)
    sweep(0, 1)
    start("v", 1)

    finish("l")

    def face(d, peer, own, weight, rows):
        for n, r in enumerate(rows):
            at = slice(r, r + 1)
            place(n * CZ, peer[at], [(own[at], weight[at])])
        depth = len(rows) * CZ
        tile = lax.dot_general(xs[:, :depth], ys[:, :depth], NT, preferred_element_type=F32)
        mf[AGG * (d + 1) : AGG * (d + 2)] = tile[:, :AGG] + tile[:, AGG:]

    def pair_rows(values):
        even = (lanes_of(values.shape) & 1) == 0
        return jnp.where(even, values, lane_roll(row_roll(values, -1), 1))

    def pair_packed(values):
        even = (lanes_of(values.shape) & 4) == 0
        return jnp.where(even, values, lane_roll(row_roll(values, -2), 4))

    for side in range(2):
        face(side, squeeze_cells(lxh[side]), squeeze_cells(lc[side * (BX - 1), TOP:END]),
             squeeze_cells(wxf[side]), range(0, CY, 4))
        face(2 + side, pair_rows(lyh[side]), pair_rows(lys[side]), pair_rows(wyf[side]), range(0, BX, 2))
        wz = fzf[side] + lane_roll(fzf[side], -4)
        wz = pair_packed(wz + row_roll(wz, -1))
        wz = jnp.where(lanes_of((8, CZ)) < 4 * CX, wz, 0.0)
        face(4 + side, pair_packed(lzh[side]), pair_packed(lzs[side]), wz, (0, 4))

    def add_rows(block, total):
        return total + mf[pl.ds(pl.multiple_of(8 * block, 8), 8), :]

    coarse_diag = jnp.sum(lax.fori_loop(0, 7 * AGG // 8, add_rows, zero_tile), axis=0, keepdims=True)
    coarse_scale = OMEGA_COARSE / coarse_diag
    square = (AGG, AGG)
    mf[0:AGG] = jnp.where(rows_of(square) == lanes_of(square), 0.0, mf[0:AGG])
    for t in range(7):
        high, low = split(mf[AGG * t : AGG * (t + 1)])
        mm[AGG * t : AGG * (t + 1), :AGG] = high.astype(BF16)
        mm[AGG * t : AGG * (t + 1), AGG:] = low.astype(BF16)

    finish("v", 1)

    def residual_step(block, carry):
        total = zero_plane
        for x in (2 * block, 2 * block + 1):
            centre, image = neighbours(1, x)
            total = total + dg[x] * (image * (1.0 / OMEGA_FINE) - centre)
        ew[0, block] = squeeze_cells(quad_sum(total))
        return carry

    lax.fori_loop(0, BX, residual_step, 0)
    wanted = rows_of((AGG, CZ)).astype(F32)

    def restrict_step(block, sums):
        for m in range(8):
            rows = slice(4 * m, 4 * m + 1)
            label = jnp.broadcast_to(el[0, block, rows], (AGG, CZ))
            value = jnp.broadcast_to(ew[0, block, rows], (AGG, CZ))
            sums = sums + jnp.where(label == wanted, value, 0.0)
        return sums

    sums = lax.fori_loop(0, BX, restrict_step, jnp.zeros((AGG, CZ), F32))
    coarse_rhs = lax.dot_general(
        jnp.ones((8, CZ), F32), sums, NT, preferred_element_type=F32, precision=lax.Precision.HIGHEST)

    small_row = rows_of((8, CZ))

    def coarse_step(turn, correction):
        slot = lax.rem(turn, 2)
        high, low = split(correction)
        tile = jnp.where(small_row == 0, high, jnp.where(small_row == 1, low, 0.0))
        cs[slot] = tile
        start("c", slot)
        image = jnp.dot(tile.astype(BF16), mm[0:AGG], preferred_element_type=F32)
        finish("c", slot)
        beside = jnp.concatenate([ch[slot, d] for d in range(6)], axis=1).astype(BF16)
        image = image + jnp.dot(beside, mm[AGG:], preferred_element_type=F32)
        image = jnp.sum(image[:, :AGG] + image[:, AGG:], axis=0, keepdims=True)
        return (1.0 - OMEGA_COARSE) * correction + coarse_scale * (coarse_rhs + image)

    correction = lax.fori_loop(0, KC - 1, coarse_step, coarse_scale * coarse_rhs)

    def lift_step(block, carry):
        index = lc[block, TOP:END].astype(jnp.int32)
        lifted = jnp.concatenate(
            [jnp.take_along_axis(correction, index[8 * g : 8 * g + 8], axis=1, mode="promise_in_bounds")
             for g in range(4)], axis=0)
        for x in (2 * block, 2 * block + 1):
            new = v[1, x + 1, TOP:END] + lifted
            v[1, x + 1, TOP:END] = new
            carry = pack(*carry, new, x)
        return carry

    low, high = lax.fori_loop(0, BX, lift_step, (zero_tile, zero_tile))
    zs[1, 0] = low
    zs[1, 1] = high

    def post_step(turn, carry):
        slot = 1 - lax.rem(turn, 2)
        start("v", slot)
        finish("v", slot)
        sweep(slot, 1 - slot)
        return carry

    lax.fori_loop(0, POST, post_step, 0)
    store = pltpu.make_async_copy(v.at[1, 1 : CX + 1, TOP:END], out_hbm, local_sem.at[0])
    store.start()
    store.wait()


def body(right_side, conductance, absorption, block_agg):
    field = (CX, CY, CZ)
    padded = (CX + 2, CY + 16, CZ)
    any_spec = pl.BlockSpec(memory_space=pl.ANY)

    def f32(*shape):
        return pltpu.VMEM(shape, F32)

    return pl.pallas_call(
        kernel,
        out_shape=jax.ShapeDtypeStruct(field, F32),
        in_specs=[any_spec] * 4,
        out_specs=any_spec,
        scratch_shapes=[
            f32(*field), f32(*field), f32(*padded), pltpu.VMEM((BX, CY // 2, CZ // 2), jnp.int32),
            f32(2, *padded), f32(6, *field), f32(*field), f32(*field), f32(BX, CY + 16, CZ),
            f32(4, BX, CY, CZ), f32(4, BX, CY, CZ),
            f32(2, 8, CZ), f32(2, 8, CZ), f32(2, CY, CZ), f32(2, 16, CZ), f32(2, 16, CZ),
            f32(2, 8, CZ), f32(2, 8, CZ), f32(2, 2, 8, CZ), f32(2, 2, 8, CZ),
            f32(2, CY, CZ), f32(2, 16, CZ), f32(2, 8, CZ),
            pltpu.VMEM((AGG, 8 * CZ), BF16), pltpu.VMEM((2 * AGG, 8 * CZ), BF16),
            f32(AGG, 2 * AGG), f32(7 * AGG, AGG), pltpu.VMEM((7 * AGG, 2 * AGG), BF16),
            f32(2, 8, CZ), f32(2, 6, 8, CZ),
            pltpu.SemaphoreType.DMA((4,)), pltpu.SemaphoreType.DMA((6, 6)), pltpu.SemaphoreType.DMA((6, 6)),
        ],
        compiler_params=pltpu.CompilerParams(collective_id=0, has_side_effects=True),
    )(right_side, conductance, absorption, block_agg)


def solution(mesh):
    spec = P("gx", "gy", "gz")
    return jax.shard_map(body, mesh=mesh, in_specs=(spec,) * 4, out_specs=spec, check_vma=False)
```

profile of v0, /device:TPU:1, one launch (start us, length us, event | category | flops | bytes accessed | tf_op | source)
XLA Modules:
  0.0 88.4 jit_solution(17642747978186598013)
XLA Ops:
  0.0 86.6 %shard_map.46 = f32[24,32,128]{2,1,0:T(8,128)} custom-call(f32[24,32,128]{2,1,0:T(8,128)} %b_hbm.1, f32[24,32,128]{2,1,0:T(8,128)} %k_hbm.1, f32[24,32,128]{2,1,0:T(8,128)} %a_hbm.1, s32[12,16,64]{2,1,0:T(8,128)} %l_hbm.1), custom_call_target="tpu_custom_call" | custom-call | tf_op jit(solution)/shard_map/pallas_call | solution.py:487
  86.6 1.8 %copy.6 = f32[24,32,128]{2,1,0:T(8,128)} copy(f32[24,32,128]{2,1,0:T(8,128)} %shard_map.46) | data formatting | bytes 786432
where the time goes:
time: 88.5 us; the launch traced here: 88.4 us
  Pallas kernels  86.6 us (98%)
  local copies, waits for them, and re-layouts  1.77 us (2%)
    pallas_call x1, Pallas kernels, body(): pl.pallas_call(kernel, out_shape=jax.ShapeDtypeStruct(field, F32), in_spe...  86.6 us

commit v1 on v0

v1 whole, which is shorter than its diff:
```python
import jax
import jax.numpy as jnp
from jax import lax
from jax.experimental import pallas as pl
from jax.experimental.pallas import tpu as pltpu
from jax.sharding import PartitionSpec as P

AGG = 128
POST = 4
KC = 8
OMEGA_FINE = 0.8
OMEGA_COARSE = 0.7
CX, CY, CZ = 24, 32, 128
BX = CX // 2
OWN_1, OWN_2 = 4, 8
TOP = 8
END = TOP + CY
AXES = ("gx", "gy", "gz")
F32 = jnp.float32
BF16 = jnp.bfloat16
NT = (((1,), (1,)), ((), ()))


def harmonic(one_side, other_side):
    summed = one_side + other_side
    return 2.0 * (one_side * other_side) / summed


def safe_harmonic(one_side, other_side):
    summed = one_side + other_side
    return 2.0 * (one_side * other_side) / jnp.where(summed > 0.0, summed, 1.0)


def lanes_of(shape):
    return lax.broadcasted_iota(jnp.int32, shape, 1)


def rows_of(shape):
    return lax.broadcasted_iota(jnp.int32, shape, 0)


def lane_roll(values, shift):
    return pltpu.roll(values, shift % CZ if isinstance(shift, int) else shift, 1)


def row_roll(values, shift):
    return pltpu.roll(values, shift % values.shape[0], 0)


def quad_sum(values):
    pair = values + row_roll(values, -1)
    return pair + lane_roll(pair, -1)


def squeeze_cells(values):
    even = (lanes_of(values.shape) & 1) == 0
    return jnp.where(even, values, lane_roll(row_roll(values, -2), 1))


def split(values):
    high = values.astype(BF16).astype(F32)
    return high, values - high


def spread_row(row):
    return jnp.broadcast_to(row, (16, CZ)).astype(BF16)


def kernel(
    b_hbm, k_hbm, a_hbm, l_hbm, out_hbm,
    bv, av, kp, lv, v, gw, c0, dg, sc, fx, fy, fz, gz, gy, gx, lc, el, ew,
    kxh, kyh, kzs, kzh, lxh, lys, lyh, lzs, lzh, xh, yh, zs, zh,
    fze, wyf, rows_y, xs, ys, acc, mf, mm, cs, ch,
    local_sem, send_sem, recv_sem,
):
    pos = [lax.axis_index(a) for a in AXES]
    size = [lax.axis_size(a) for a in AXES]
    has = []
    dev = []
    for axis in range(3):
        has.append(pos[axis] > 0)
        dev.append({AXES[axis]: pos[axis] - 1})
        has.append(pos[axis] < size[axis] - 1)
        dev.append({AXES[axis]: pos[axis] + 1})
    cells = slice(TOP, END)

    def exchange_of(kind, slot):
        if kind == "k":
            src = [kp.at[1, cells], kp.at[CX, cells], kp.at[1 : CX + 1, TOP : TOP + 1],
                   kp.at[1 : CX + 1, END - 1 : END], kzs.at[0], kzs.at[1]]
            dst = [kxh.at[0], kxh.at[1], kyh.at[0, :, 0:1], kyh.at[1, :, 7:8], kzh.at[0], kzh.at[1]]
            sem = 0
        elif kind == "l":
            src = [lc.at[0, cells], lc.at[BX - 1, cells], lys.at[0], lys.at[1], lzs.at[0], lzs.at[1]]
            dst = [lxh.at[0], lxh.at[1], lyh.at[0], lyh.at[1], lzh.at[0], lzh.at[1]]
            sem = 1
        elif kind == "v":
            src = [v.at[slot, 1, cells], v.at[slot, CX, cells], v.at[slot, 1 : CX + 1, TOP : TOP + 1],
                   v.at[slot, 1 : CX + 1, END - 1 : END], zs.at[slot, 0], zs.at[slot, 1]]
            dst = [xh.at[slot, 0], xh.at[slot, 1], yh.at[slot, 0, :, 0:1], yh.at[slot, 1, :, 7:8],
                   zh.at[slot, 0], zh.at[slot, 1]]
            sem = 2 + slot
        else:
            src = [cs.at[slot]] * 6
            dst = [ch.at[slot, d] for d in range(6)]
            sem = 4 + slot
        return src, dst, sem

    def copy_to(kind, slot, d):
        src, dst, sem = exchange_of(kind, slot)
        return pltpu.make_async_remote_copy(
            src[d], dst[d ^ 1], send_sem.at[sem, d], recv_sem.at[sem, d ^ 1],
            device_id=dev[d], device_id_type=pl.DeviceIdType.MESH)

    def copy_from(kind, slot, d):
        src, dst, sem = exchange_of(kind, slot)
        return pltpu.make_async_remote_copy(
            src[d], dst[d], send_sem.at[sem, d], recv_sem.at[sem, d],
            device_id=dev[d], device_id_type=pl.DeviceIdType.MESH)

    def start(kind, slot=0, sides=(4, 5, 2, 3, 0, 1)):
        for d in sides:
            @pl.when(has[d])
            def _():
                copy_to(kind, slot, d).start()

    def finish(kind, slot=0):
        for d in range(6):
            @pl.when(has[d])
            def _():
                copy_from(kind, slot, d).wait_recv()
        for d in range(6):
            @pl.when(has[d])
            def _():
                copy_to(kind, slot, d).wait_send()

    load_k = pltpu.make_async_copy(k_hbm, kp.at[1 : CX + 1, cells], local_sem.at[0])
    load_l = pltpu.make_async_copy(l_hbm, lv, local_sem.at[1])
    load_a = pltpu.make_async_copy(a_hbm, av, local_sem.at[2])
    load_b = pltpu.make_async_copy(b_hbm, bv, local_sem.at[3])
    load_k.start()
    load_l.start()
    load_a.start()
    load_b.start()

    zero_plane = jnp.zeros((CY, CZ), F32)
    zero_tile = jnp.zeros((8, CZ), F32)
    for side in range(2):
        kxh[side] = zero_plane
        lxh[side] = zero_plane
        lyh[side] = jnp.zeros((16, CZ), F32)
        for half in range(2):
            kzh[side, half] = zero_tile
            lzh[side, half] = zero_tile
        for x in range(CX):
            kyh[side, x] = zero_tile

    barrier = pltpu.get_barrier_semaphore()
    count = jnp.int32(0)
    for d in range(6):
        @pl.when(has[d])
        def _():
            pl.semaphore_signal(barrier, inc=1, device_id=dev[d], device_id_type=pl.DeviceIdType.MESH)
        count = count + has[d].astype(jnp.int32)

    for slot in range(2):
        for d in range(6):
            ch[slot, d] = zero_tile
        for side in range(2):
            xh[slot, side] = zero_plane
            for half in range(2):
                zh[slot, side, half] = zero_tile
            for x in range(CX):
                yh[slot, side, x] = zero_tile
        for edge in (0, CX + 1):
            v[slot, edge, cells] = zero_plane
        for x in range(CX):
            v[slot, x + 1, TOP - 8 : TOP] = zero_tile
            v[slot, x + 1, END : END + 8] = zero_tile
    for edge in (0, CX + 1):
        kp[edge, cells] = zero_plane
    for x in range(CX):
        kp[x + 1, TOP - 8 : TOP] = zero_tile
        kp[x + 1, END : END + 8] = zero_tile
        fy[x, CY : CY + 8] = zero_tile
    fx[0] = zero_plane
    for side in range(2):
        lys[side] = jnp.zeros((16, CZ), F32)
        wyf[side] = jnp.zeros((16, CZ), F32)
        rows_y[side] = jnp.zeros((16, CZ), F32)
    pl.semaphore_wait(barrier, count)

    lane_8 = lanes_of((8, CZ))
    rim = (lane_8 == 0) | (lane_8 == CZ - 1)
    odd = (lane_8 & 1) == 1

    def pack_plane(packed, plane, x):
        for g in range(4):
            piece = jnp.where(rim, plane[8 * g : 8 * g + 8], 0.0)
            packed = packed + lane_roll(piece, 2 * (4 * x + g))
        return packed

    def store_packed(ref, half, packed):
        ref[0, half] = lane_roll(packed, -1)
        ref[1, half] = lane_roll(packed, 1)

    def joined(ref, half):
        return jnp.where(odd, ref[1, half], ref[0, half])

    def unpack_plane(packed, x):
        return [lane_roll(packed, -2 * (4 * x + g)) for g in range(4)]

    load_k.wait()
    start("k", 0, range(4))
    own_k = []
    for half in range(2):
        packed = zero_tile
        for x in range(12):
            packed = pack_plane(packed, kp[12 * half + x + 1, cells], x)
        store_packed(kzs, half, packed)
        own_k.append(packed)
    start("k", 0, (4, 5))

    load_l.wait()
    labels = lv[...].reshape(BX * 16, 64).astype(F32).astype(BF16)
    widen = jnp.where(lanes_of((64, CZ)) // 2 == rows_of((64, CZ)), 1.0, 0.0).astype(BF16)
    wide = jnp.dot(labels, widen, preferred_element_type=F32).astype(BF16)
    tall_shape = (BX * CY, BX * 16)
    heighten = jnp.where(rows_of(tall_shape) // 2 == lanes_of(tall_shape), 1.0, 0.0).astype(BF16)
    tall = jnp.dot(heighten, wide, preferred_element_type=F32)
    for x in range(BX):
        lc[x, cells] = tall[x * CY : (x + 1) * CY]
        lc[x, END : END + 8] = zero_tile
        lys[0, x : x + 1] = tall[x * CY : x * CY + 1]
        lys[1, x : x + 1] = tall[x * CY + CY - 1 : x * CY + CY]
    own_l = []
    for half in range(2):
        packed = zero_tile
        for x in range(6):
            plane = lc[6 * half + x, cells]
            packed = pack_plane(packed, plane, 2 * x)
            packed = pack_plane(packed, plane, 2 * x + 1)
        store_packed(lzs, half, packed)
        own_l.append(packed)
    start("l")

    lane = lanes_of((CY, CZ))
    row = rows_of((CY, CZ))
    load_a.wait()

    def faces(x, fx_low):
        centre = kp[x + 1, cells]
        fx_high = harmonic(centre, kp[x + 2, cells])
        fy_low = harmonic(kp[x + 1, TOP - 1 : END - 1], centre)
        fy[x, 0:CY] = fy_low
        fz_low = jnp.where(lane == 0, 0.0, harmonic(lane_roll(centre, 1), centre))
        fz_high = lane_roll(fz_low, -1)
        fy_high = fy[x, 1 : CY + 1]
        fx[x + 1] = fx_high
        fz[0, x] = fz_low
        fz[1, x] = fz_high
        dg[x] = av[x] + fx_low + fx_high + fy_low + fy_high + fz_low + fz_high
        return fx_high, fy_high, fz_high

    def block_step(block, fx_low):
        x = 2 * block
        fx_mid, fy_high_0, fz_high_0 = faces(x, fx_low)
        fx_high, fy_high_1, fz_high_1 = faces(x + 1, fx_mid)
        wx = quad_sum(fx_high)
        wy = fy_high_0 + fy_high_1
        wy = row_roll(wy + lane_roll(wy, -1), -1)
        wz = fz_high_0 + fz_high_1
        wz = lane_roll(wz + row_roll(wz, -1), -1)
        wa = 0.5 * quad_sum(av[x] + av[x + 1])
        own = lc[block, cells]
        lx = lc[jnp.minimum(block + 1, BX - 1), cells]
        ly = lc[block, TOP + 2 : END + 2]
        lz = lane_roll(own, -2)
        lx = jnp.where(lx == own, -1.0, lx)
        ly = jnp.where((ly == own) | (row >= CY - 2), -1.0, ly)
        lz = jnp.where((lz == own) | (lane >= CZ - 2), -1.0, lz)
        same = ly == lx
        wx = wx + jnp.where(same, wy, 0.0)
        ly = jnp.where(same, -1.0, ly)
        same = lz == lx
        wx = wx + jnp.where(same, wz, 0.0)
        lz = jnp.where(same, -1.0, lz)
        same = lz == ly
        wy = wy + jnp.where(same, wz, 0.0)
        lz = jnp.where(same, -1.0, lz)
        for n, field in enumerate((own, lx, ly, lz)):
            el[n, block] = squeeze_cells(field)
        for n, field in enumerate((wa, wx, wy, wz)):
            ew[n, block] = squeeze_cells(field)
        return fx_high

    def block_pair(turn, fx_low):
        return block_step(2 * turn + 1, block_step(2 * turn, fx_low))

    lax.fori_loop(0, BX // 2, block_pair, zero_plane)

    number = rows_of((16, CZ)).astype(F32)
    numbers = [(number + 16.0 * q).astype(BF16) for q in range(8)]
    one = jnp.ones((16, CZ), BF16)
    zero = jnp.zeros((16, CZ), BF16)

    def place(at, lhs_label, pairs):
        lhs_label = spread_row(lhs_label)
        spread = []
        for label, weight in pairs:
            high, low = split(weight)
            spread.append((spread_row(label), spread_row(high), spread_row(low)))
        for q in range(8):
            xs[16 * q : 16 * q + 16, at : at + CZ] = jnp.where(lhs_label == numbers[q], one, zero)
            y_high = zero
            y_low = zero
            for label, high, low in spread:
                hit = label == numbers[q]
                y_high = jnp.where(hit, high, y_high)
                y_low = jnp.where(hit, low, y_low)
            ys[16 * q : 16 * q + 16, at : at + CZ] = y_high
            ys[AGG + 16 * q : AGG + 16 * q + 16, at : at + CZ] = y_low

    acc[...] = jnp.zeros((AGG, 2 * AGG), F32)

    def own_step(block, carry):
        for m in range(8):
            at = slice(4 * m, 4 * m + 1)
            pairs = [(el[n, block, at], ew[n, block, at]) for n in range(4)]
            place(m * CZ, pairs[0][0], pairs)
        acc[...] += lax.dot_general(xs[...], ys[...], NT, preferred_element_type=F32)
        return carry

    lax.fori_loop(0, OWN_1, own_step, 0)
    load_b.wait()
    finish("k")

    gx[0] = harmonic(kp[1, cells], kxh[0])
    gx[1] = harmonic(kp[CX, cells], kxh[1])
    for half in range(2):
        fze[half] = safe_harmonic(own_k[half], joined(kzh, half))

    def first_step(half, carry):
        packed = zero_tile
        face_z = fze[half]
        for local in range(12):
            x = 12 * half + local
            wall = unpack_plane(face_z, local)
            wall = jnp.concatenate([jnp.where(rim, w, 0.0) for w in wall], axis=0)
            gz[x] = wall
            low = harmonic(kp[x + 1, TOP : TOP + 8], kyh[0, x])
            high = harmonic(kp[x + 1, END - 8 : END], kyh[1, x])
            gy[0, x] = low
            gy[1, x] = high
            diag = dg[x] + wall + jnp.concatenate([low, jnp.zeros((16, CZ), F32), high], axis=0)
            if local == 0:
                diag = diag + jnp.where(half == 0, gx[0], 0.0)
            if local == 11:
                diag = diag + jnp.where(half == 1, gx[1], 0.0)
            scale = OMEGA_FINE / diag
            first = scale * bv[x]
            dg[x] = diag
            sc[x] = scale
            c0[x] = first
            v[0, x + 1, cells] = first
            packed = pack_plane(packed, first, local)
        store_packed(zs.at[0], half, packed)
        return carry

    lax.fori_loop(0, 2, first_step, 0)
    start("v", 0)

    def face_rows(block, carry):
        x = 2 * block
        low = (gy[0, x] + gy[0, x + 1])[0:1]
        high = (gy[1, x] + gy[1, x + 1])[7:8]
        wyf[0, pl.ds(block, 1)] = low + lane_roll(low, -1)
        wyf[1, pl.ds(block, 1)] = high + lane_roll(high, -1)
        return carry

    lax.fori_loop(0, BX, face_rows, 0, unroll=True)
    wxf = [quad_sum(gx[side]) for side in range(2)]

    def scale_step(turn, carry):
        for local in range(4):
            x = 4 * turn + local
            scale = sc[x]
            gw[0, x] = scale * fx[x]
            gw[1, x] = scale * fx[x + 1]
            gw[2, x] = scale * fy[x, 0:CY]
            gw[3, x] = scale * fy[x, 1 : CY + 1]
            gw[4, x] = scale * fz[0, x]
            gw[5, x] = scale * fz[1, x]
            gz[x] = scale * gz[x]
            gy[0, x] = scale[0:8] * gy[0, x]
            gy[1, x] = scale[CY - 8 :] * gy[1, x]
        return carry

    lax.fori_loop(0, CX // 4, scale_step, 0)
    gx[0] = sc[0] * gx[0]
    gx[1] = sc[CX - 1] * gx[1]

    def inner(slot, other):
        def step(turn, carry):
            for local in range(4):
                x = 4 * turn + local
                centre = v[slot, x + 1, cells]
                total = c0[x] + (1.0 - OMEGA_FINE) * centre
                total = total + gw[0, x] * v[slot, x, cells] + gw[1, x] * v[slot, x + 2, cells]
                total = total + gw[2, x] * v[slot, x + 1, TOP - 1 : END - 1]
                total = total + gw[3, x] * v[slot, x + 1, TOP + 1 : END + 1]
                total = total + gw[4, x] * lane_roll(centre, 1) + gw[5, x] * lane_roll(centre, -1)
                v[other, x + 1, cells] = total
            return carry

        lax.fori_loop(0, CX // 4, step, 0)

    def outer(slot, other):
        v[other, 1, cells] += gx[0] * xh[slot, 0]
        v[other, CX, cells] += gx[1] * xh[slot, 1]

        def step(half, carry):
            packed = zero_tile
            halo_z = joined(zh.at[slot], half)
            for local in range(12):
                x = 12 * half + local
                wall = jnp.concatenate(unpack_plane(halo_z, local), axis=0)
                low = gy[0, x] * yh[slot, 0, x]
                high = gy[1, x] * yh[slot, 1, x]
                new = v[other, x + 1, cells] + gz[x] * wall
                new = new + jnp.concatenate([low, jnp.zeros((16, CZ), F32), high], axis=0)
                v[other, x + 1, cells] = new
                packed = pack_plane(packed, new, local)
            store_packed(zs.at[other], half, packed)
            return carry

        lax.fori_loop(0, 2, step, 0)

    inner(0, 1)
    lax.fori_loop(OWN_1, OWN_2, own_step, 0)

    finish("v", 0)
    outer(0, 1)
    start("v", 1)

    lax.fori_loop(OWN_2, BX, own_step, 0)
    sum_own = acc[:, :AGG] + acc[:, AGG:]
    mf[0:AGG] = sum_own + sum_own.T
    finish("l")

    def pair_rows(values):
        return jnp.where((lanes_of(values.shape) & 1) == 0, values, lane_roll(row_roll(values, -1), 1))

    def face_blocks(halves, side, summed):
        out = []
        for values in halves:
            if side:
                values = lane_roll(values, 1)
            if summed:
                values = values + lane_roll(values, -8)
                values = values + row_roll(values, -1)
            out.append(jnp.where((lane_8 & 8) == 0, values, lane_roll(row_roll(values, -2), 8)))
        out = jnp.where(odd, lane_roll(out[1], 1), out[0])
        return jnp.where(lane_8 < 96, out, 0.0) if summed else out

    faces_of = []
    for side in range(2):
        faces_of.append((side, squeeze_cells(lxh[side]), squeeze_cells(lc[side * (BX - 1), cells]),
                         squeeze_cells(wxf[side]), range(0, CY, 4)))
        faces_of.append((2 + side, pair_rows(lyh[side]), pair_rows(lys[side]), pair_rows(wyf[side]), range(0, BX, 2)))
        peers = [joined(lzh, half) for half in range(2)]
        faces_of.append((4 + side, face_blocks(peers, side, False), face_blocks(own_l, side, False),
                         face_blocks([fze[0], fze[1]], side, True), (0, 4)))

    for d, peer, own, weight, at_rows in faces_of:
        for n, r in enumerate(at_rows):
            at = slice(r, r + 1)
            place(n * CZ, peer[at], [(own[at], weight[at])])
        depth = len(at_rows) * CZ
        tile = lax.dot_general(xs[:, :depth], ys[:, :depth], NT, preferred_element_type=F32)
        mf[AGG * (d + 1) : AGG * (d + 2)] = tile[:, :AGG] + tile[:, AGG:]

    column = zero_tile
    for r in range(0, 7 * AGG, 8):
        column = column + mf[r : r + 8]
    coarse_diag = jnp.sum(column, axis=0, keepdims=True)
    coarse_scale = OMEGA_COARSE / coarse_diag
    square = (AGG, AGG)
    mf[0:AGG] = jnp.where(rows_of(square) == lanes_of(square), 0.0, mf[0:AGG])
    for t in range(7):
        high, low = split(mf[AGG * t : AGG * (t + 1)])
        mm[AGG * t : AGG * (t + 1), :AGG] = high.astype(BF16)
        mm[AGG * t : AGG * (t + 1), AGG:] = low.astype(BF16)

    inner(1, 0)

    def residual_step(turn, carry):
        for local in range(4):
            block = 4 * turn + local
            total = zero_plane
            for x in (2 * block, 2 * block + 1):
                total = total + dg[x] * (v[0, x + 1, cells] - v[1, x + 1, cells])
            ew[0, block] = squeeze_cells(quad_sum(total * (1.0 / OMEGA_FINE)))
        return carry

    lax.fori_loop(0, BX // 4, residual_step, 0)
    wanted = rows_of((AGG, CZ)).astype(F32)

    def gather_row(sums, label, value):
        label = jnp.broadcast_to(label, (AGG, CZ))
        return sums + jnp.where(label == wanted, jnp.broadcast_to(value, (AGG, CZ)), 0.0)

    def restrict_step(block, sums):
        for m in range(8):
            at = slice(4 * m, 4 * m + 1)
            sums = gather_row(sums, el[0, block, at], ew[0, block, at])
        return sums

    sums = lax.fori_loop(0, BX, restrict_step, jnp.zeros((AGG, CZ), F32))

    finish("v", 1)
    halo_z = [fze[half] * joined(zh.at[1], half) for half in range(2)]
    inverse = 1.0 / OMEGA_FINE
    for block in range(BX):
        x = 2 * block
        low = sum(gy[0, n] * yh[1, 0, n] * dg[n, 0:8] for n in (x, x + 1))[0:1]
        high = sum(gy[1, n] * yh[1, 1, n] * dg[n, CY - 8 : CY] for n in (x, x + 1))[7:8]
        rows_y[0, block : block + 1] = inverse * (low + lane_roll(low, -1))
        rows_y[1, block : block + 1] = inverse * (high + lane_roll(high, -1))
    for side in range(2):
        plane = gx[side] * xh[1, side] * dg[side * (CX - 1)] * inverse
        values = (squeeze_cells(quad_sum(plane)), pair_rows(rows_y[side]), face_blocks(halo_z, side, True))
        for (d, peer, own, weight, at_rows), value in zip(faces_of[3 * side : 3 * side + 3], values):
            for r in at_rows:
                sums = gather_row(sums, own[r : r + 1], value[r : r + 1])
    coarse_rhs = lax.dot_general(
        jnp.ones((8, CZ), F32), sums, NT, preferred_element_type=F32, precision=lax.Precision.HIGHEST)

    small_row = rows_of((8, CZ))

    def coarse_step(turn, correction):
        slot = lax.rem(turn, 2)
        high, low = split(correction)
        tile = jnp.where(small_row == 0, high, jnp.where(small_row == 1, low, 0.0))
        cs[slot] = tile
        start("c", slot)
        image = jnp.dot(tile.astype(BF16), mm[0:AGG], preferred_element_type=F32)
        base = (1.0 - OMEGA_COARSE) * correction + coarse_scale * coarse_rhs
        finish("c", slot)
        beside = jnp.concatenate([ch[slot, d] for d in range(6)], axis=1).astype(BF16)
        image = image + jnp.dot(beside, mm[AGG:], preferred_element_type=F32)
        image = jnp.sum(image[:, :AGG] + image[:, AGG:], axis=0, keepdims=True)
        return base + coarse_scale * image

    correction = lax.fori_loop(0, KC - 1, coarse_step, coarse_scale * coarse_rhs)

    def lift_step(half, carry):
        packed = zero_tile
        for local in range(6):
            block = 6 * half + local
            index = lc[block, cells].astype(jnp.int32)
            lifted = jnp.concatenate(
                [jnp.take_along_axis(correction, index[8 * g : 8 * g + 8], axis=1, mode="promise_in_bounds")
                 for g in range(4)], axis=0)
            for n in range(2):
                x = 2 * block + n
                new = v[1, x + 1, cells] + lifted
                v[1, x + 1, cells] = new
                packed = pack_plane(packed, new, 2 * local + n)
        store_packed(zs.at[1], half, packed)
        return carry

    lax.fori_loop(0, 2, lift_step, 0)

    def post_step(turn, carry):
        slot = 1 - lax.rem(turn, 2)
        start("v", slot)
        inner(slot, 1 - slot)
        finish("v", slot)
        outer(slot, 1 - slot)
        return carry

    lax.fori_loop(0, POST, post_step, 0)
    store = pltpu.make_async_copy(v.at[1, 1 : CX + 1, cells], out_hbm, local_sem.at[0])
    store.start()
    store.wait()


def body(right_side, conductance, absorption, block_agg):
    field = (CX, CY, CZ)
    padded = (CX + 2, CY + 16, CZ)
    any_spec = pl.BlockSpec(memory_space=pl.ANY)

    def f32(*shape):
        return pltpu.VMEM(shape, F32)

    scratch = dict(
        bv=f32(*field), av=f32(*field), kp=f32(*padded), lv=pltpu.VMEM((BX, CY // 2, CZ // 2), jnp.int32),
        v=f32(2, *padded), gw=f32(6, *field), c0=f32(*field), dg=f32(*field), sc=f32(*field),
        fx=f32(CX + 1, CY, CZ), fy=f32(CX, CY + 8, CZ), fz=f32(2, *field),
        gz=f32(*field), gy=f32(2, CX, 8, CZ), gx=f32(2, CY, CZ),
        lc=f32(BX, CY + 16, CZ), el=f32(4, BX, CY, CZ), ew=f32(4, BX, CY, CZ),
        kxh=f32(2, CY, CZ), kyh=f32(2, CX, 8, CZ), kzs=f32(2, 2, 8, CZ), kzh=f32(2, 2, 8, CZ),
        lxh=f32(2, CY, CZ), lys=f32(2, 16, CZ), lyh=f32(2, 16, CZ), lzs=f32(2, 2, 8, CZ), lzh=f32(2, 2, 8, CZ),
        xh=f32(2, 2, CY, CZ), yh=f32(2, 2, CX, 8, CZ), zs=f32(2, 2, 2, 8, CZ), zh=f32(2, 2, 2, 8, CZ),
        fze=f32(2, 8, CZ), wyf=f32(2, 16, CZ), rows_y=f32(2, 16, CZ),
        xs=pltpu.VMEM((AGG, 8 * CZ), BF16), ys=pltpu.VMEM((2 * AGG, 8 * CZ), BF16),
        acc=f32(AGG, 2 * AGG), mf=f32(7 * AGG, AGG), mm=pltpu.VMEM((7 * AGG, 2 * AGG), BF16),
        cs=f32(2, 8, CZ), ch=f32(2, 6, 8, CZ),
    )
    return pl.pallas_call(
        kernel,
        out_shape=jax.ShapeDtypeStruct(field, F32),
        in_specs=[any_spec] * 4,
        out_specs=any_spec,
        scratch_shapes=list(scratch.values()) + [
            pltpu.SemaphoreType.DMA((4,)), pltpu.SemaphoreType.DMA((6, 6)), pltpu.SemaphoreType.DMA((6, 6)),
        ],
        compiler_params=pltpu.CompilerParams(collective_id=0, has_side_effects=True),
    )(right_side, conductance, absorption, block_agg)


def solution(mesh):
    spec = P("gx", "gy", "gz")
    return jax.shard_map(body, mesh=mesh, in_specs=(spec,) * 4, out_specs=spec, check_vma=False)
```

time: 88.5 us -> 63.5 us (0.72)
  Pallas kernels: 86.6 us -> 61.6 us
    pallas_call x1, Pallas kernels: 86.6 us -> 61.6 us  [body(): pl.pallas_call(kernel, out_shape=jax.ShapeDtypeStruct(field, F32), in_spe...]
where the time goes in v1:
time: 63.5 us; the launch traced here: 63.4 us
  Pallas kernels  61.6 us (97%)
  local copies, waits for them, and re-layouts  1.77 us (3%)
    pallas_call x1, Pallas kernels, body(): pl.pallas_call(kernel, out_shape=jax.ShapeDtypeStruct(field, F32), in_spe...  61.6 us
    unnamed x1, local copies, waits for them, and re-layouts  1.77 us

profile of v1, /device:TPU:1, one launch (start us, length us, event | category | flops | bytes accessed | tf_op | source)
XLA Modules:
  0.0 63.4 jit_solution(3261960261555652039)
XLA Ops:
  0.0 61.6 %shard_map.46 = f32[24,32,128]{2,1,0:T(8,128)} custom-call(f32[24,32,128]{2,1,0:T(8,128)} %b_hbm.1, f32[24,32,128]{2,1,0:T(8,128)} %k_hbm.1, f32[24,32,128]{2,1,0:T(8,128)} %a_hbm.1, s32[12,16,64]{2,1,0:T(8,128)} %l_hbm.1), custom_call_target="tpu_custom_call" | custom-call | tf_op jit(solution)/shard_map/pallas_call | solution.py:611
  61.6 1.8 %copy.6 = f32[24,32,128]{2,1,0:T(8,128)} copy(f32[24,32,128]{2,1,0:T(8,128)} %shard_map.46) | data formatting | bytes 786432

commit v2 on v1

--- a/solution.py
+++ b/solution.py
@@ -70,7 +70,7 @@
     b_hbm, k_hbm, a_hbm, l_hbm, out_hbm,
     bv, av, kp, lv, v, gw, c0, dg, sc, fx, fy, fz, gz, gy, gx, lc, el, ew,
     kxh, kyh, kzs, kzh, lxh, lys, lyh, lzs, lzh, xh, yh, zs, zh,
-    fze, wyf, rows_y, xs, ys, acc, mf, mm, cs, ch,
+    fze, wyf, rows_y, zp, gzp, hz, xs, ys, acc, mf, mm, cs, ch,
     local_sem, send_sem, recv_sem,
 ):
     pos = [lax.axis_index(a) for a in AXES]
@@ -124,15 +124,21 @@
             def _():
                 copy_to(kind, slot, d).start()
 
-    def finish(kind, slot=0):
+    def finish_send(kind, slot=0):
+        for d in range(6):
+            @pl.when(has[d])
+            def _():
+                copy_to(kind, slot, d).wait_send()
+
+    def finish_recv(kind, slot=0):
         for d in range(6):
             @pl.when(has[d])
             def _():
                 copy_from(kind, slot, d).wait_recv()
-        for d in range(6):
-            @pl.when(has[d])
-            def _():
-                copy_to(kind, slot, d).wait_send()
+
+    def finish(kind, slot=0):
+        finish_send(kind, slot)
+        finish_recv(kind, slot)
 
     load_k = pltpu.make_async_copy(k_hbm, kp.at[1 : CX + 1, cells], local_sem.at[0])
     load_l = pltpu.make_async_copy(l_hbm, lv, local_sem.at[1])
@@ -188,7 +194,6 @@
         lys[side] = jnp.zeros((16, CZ), F32)
         wyf[side] = jnp.zeros((16, CZ), F32)
         rows_y[side] = jnp.zeros((16, CZ), F32)
-    pl.semaphore_wait(barrier, count)
 
     lane_8 = lanes_of((8, CZ))
     rim = (lane_8 == 0) | (lane_8 == CZ - 1)
@@ -211,7 +216,6 @@
         return [lane_roll(packed, -2 * (4 * x + g)) for g in range(4)]
 
     load_k.wait()
-    start("k", 0, range(4))
     own_k = []
     for half in range(2):
         packed = zero_tile
@@ -219,7 +223,8 @@
             packed = pack_plane(packed, kp[12 * half + x + 1, cells], x)
         store_packed(kzs, half, packed)
         own_k.append(packed)
-    start("k", 0, (4, 5))
+    pl.semaphore_wait(barrier, count)
+    start("k")
 
     load_l.wait()
     labels = lv[...].reshape(BX * 16, 64).astype(F32).astype(BF16)
@@ -400,10 +405,20 @@
     gx[0] = sc[0] * gx[0]
     gx[1] = sc[CX - 1] * gx[1]
 
+    def pack_scale(half, carry):
+        packed = zero_tile
+        for local in range(12):
+            packed = pack_plane(packed, gz[12 * half + local], local)
+        gzp[half] = packed
+        return carry
+
+    lax.fori_loop(0, 2, pack_scale, 0)
+
     def inner(slot, other):
-        def step(turn, carry):
-            for local in range(4):
-                x = 4 * turn + local
+        def step(half, carry):
+            packed = zero_tile
+            for local in range(12):
+                x = 12 * half + local
                 centre = v[slot, x + 1, cells]
                 total = c0[x] + (1.0 - OMEGA_FINE) * centre
                 total = total + gw[0, x] * v[slot, x, cells] + gw[1, x] * v[slot, x + 2, cells]
@@ -411,17 +426,34 @@
                 total = total + gw[3, x] * v[slot, x + 1, TOP + 1 : END + 1]
                 total = total + gw[4, x] * lane_roll(centre, 1) + gw[5, x] * lane_roll(centre, -1)
                 v[other, x + 1, cells] = total
+                packed = pack_plane(packed, total, local)
+            zp[half] = packed
             return carry
 
-        lax.fori_loop(0, CX // 4, step, 0)
-
-    def outer(slot, other):
+        lax.fori_loop(0, 2, step, 0)
+
+    def outer_faces(slot, other):
+        for half in range(2):
+            halo_z = joined(zh.at[slot], half)
+            hz[half] = halo_z
+            packed = zp[half] + gzp[half] * halo_z
+            for local in range(12):
+                x = 12 * half + local
+                low = jnp.where(rim, gy[0, x] * yh[slot, 0, x], 0.0)
+                high = jnp.where(rim, gy[1, x] * yh[slot, 1, x], 0.0)
+                packed = packed + lane_roll(low, 8 * local) + lane_roll(high, 8 * local + 6)
+            if half == 0:
+                packed = pack_plane(packed, gx[0] * xh[slot, 0], 0)
+            else:
+                packed = pack_plane(packed, gx[1] * xh[slot, 1], 11)
+            store_packed(zs.at[other], half, packed)
+
+    def outer_rest(slot, other):
         v[other, 1, cells] += gx[0] * xh[slot, 0]
         v[other, CX, cells] += gx[1] * xh[slot, 1]
 
         def step(half, carry):
-            packed = zero_tile
-            halo_z = joined(zh.at[slot], half)
+            halo_z = hz[half]
             for local in range(12):
                 x = 12 * half + local
                 wall = jnp.concatenate(unpack_plane(halo_z, local), axis=0)
@@ -430,8 +462,6 @@
                 new = v[other, x + 1, cells] + gz[x] * wall
                 new = new + jnp.concatenate([low, jnp.zeros((16, CZ), F32), high], axis=0)
                 v[other, x + 1, cells] = new
-                packed = pack_plane(packed, new, local)
-            store_packed(zs.at[other], half, packed)
             return carry
 
         lax.fori_loop(0, 2, step, 0)
@@ -440,8 +470,10 @@
     lax.fori_loop(OWN_1, OWN_2, own_step, 0)
 
     finish("v", 0)
-    outer(0, 1)
-    start("v", 1)
+    outer_faces(0, 1)
+    start("v", 1, (4, 5))
+    outer_rest(0, 1)
+    start("v", 1, (2, 3, 0, 1))
 
     lax.fori_loop(OWN_2, BX, own_step, 0)
     sum_own = acc[:, :AGG] + acc[:, AGG:]
@@ -488,7 +520,7 @@
     square = (AGG, AGG)
     mf[0:AGG] = jnp.where(rows_of(square) == lanes_of(square), 0.0, mf[0:AGG])
     for t in range(7):
-        high, low = split(mf[AGG * t : AGG * (t + 1)])
+        high, low = split(mf[AGG * t : AGG * (t + 1)] * coarse_scale)
         mm[AGG * t : AGG * (t + 1), :AGG] = high.astype(BF16)
         mm[AGG * t : AGG * (t + 1), AGG:] = low.astype(BF16)
 
@@ -533,26 +565,32 @@
         for (d, peer, own, weight, at_rows), value in zip(faces_of[3 * side : 3 * side + 3], values):
             for r in at_rows:
                 sums = gather_row(sums, own[r : r + 1], value[r : r + 1])
-    coarse_rhs = lax.dot_general(
-        jnp.ones((8, CZ), F32), sums, NT, preferred_element_type=F32, precision=lax.Precision.HIGHEST)
-
-    small_row = rows_of((8, CZ))
+    high, low = split(sums)
+    ones = jnp.ones((16, CZ), BF16)
+    coarse_rhs = lax.dot_general(ones, high.astype(BF16), NT, preferred_element_type=F32)
+    coarse_rhs = coarse_rhs + lax.dot_general(ones, low.astype(BF16), NT, preferred_element_type=F32)
+    first_correction = coarse_scale * coarse_rhs[0:8]
+
+    def halves(values):
+        high, low = split(values)
+        return jnp.concatenate([high, low], axis=0).astype(BF16)
+
+    def both(values):
+        values = values[:, :AGG] + values[:, AGG:]
+        return values[0:8] + values[8:16]
 
     def coarse_step(turn, correction):
         slot = lax.rem(turn, 2)
-        high, low = split(correction)
-        tile = jnp.where(small_row == 0, high, jnp.where(small_row == 1, low, 0.0))
-        cs[slot] = tile
+        cs[slot] = correction
         start("c", slot)
-        image = jnp.dot(tile.astype(BF16), mm[0:AGG], preferred_element_type=F32)
-        base = (1.0 - OMEGA_COARSE) * correction + coarse_scale * coarse_rhs
+        image = jnp.dot(halves(correction), mm[0:AGG], preferred_element_type=F32)
+        base = (1.0 - OMEGA_COARSE) * correction + first_correction
+        base = base + both(image)
         finish("c", slot)
-        beside = jnp.concatenate([ch[slot, d] for d in range(6)], axis=1).astype(BF16)
-        image = image + jnp.dot(beside, mm[AGG:], preferred_element_type=F32)
-        image = jnp.sum(image[:, :AGG] + image[:, AGG:], axis=0, keepdims=True)
-        return base + coarse_scale * image
-
-    correction = lax.fori_loop(0, KC - 1, coarse_step, coarse_scale * coarse_rhs)
+        beside = jnp.concatenate([ch[slot, d] for d in range(6)], axis=1)
+        return base + both(jnp.dot(halves(beside), mm[AGG:], preferred_element_type=F32))
+
+    correction = lax.fori_loop(0, KC - 1, coarse_step, first_correction)
 
     def lift_step(half, carry):
         packed = zero_tile
@@ -574,13 +612,30 @@
 
     def post_step(turn, carry):
         slot = 1 - lax.rem(turn, 2)
-        start("v", slot)
+
+        @pl.when(turn > 0)
+        def _():
+            finish_send("v", 1 - slot)
+
         inner(slot, 1 - slot)
-        finish("v", slot)
-        outer(slot, 1 - slot)
-        return carry
-
+        finish_recv("v", slot)
+        outer_faces(slot, 1 - slot)
+
+        @pl.when(turn < POST - 1)
+        def _():
+            start("v", 1 - slot, (4, 5))
+
+        outer_rest(slot, 1 - slot)
+
+        @pl.when(turn < POST - 1)
+        def _():
+            start("v", 1 - slot, (2, 3, 0, 1))
+
+        return carry
+
+    start("v", 1)
     lax.fori_loop(0, POST, post_step, 0)
+    finish_send("v", 0)
     store = pltpu.make_async_copy(v.at[1, 1 : CX + 1, cells], out_hbm, local_sem.at[0])
     store.start()
     store.wait()
@@ -603,7 +658,7 @@
         kxh=f32(2, CY, CZ), kyh=f32(2, CX, 8, CZ), kzs=f32(2, 2, 8, CZ), kzh=f32(2, 2, 8, CZ),
         lxh=f32(2, CY, CZ), lys=f32(2, 16, CZ), lyh=f32(2, 16, CZ), lzs=f32(2, 2, 8, CZ), lzh=f32(2, 2, 8, CZ),
         xh=f32(2, 2, CY, CZ), yh=f32(2, 2, CX, 8, CZ), zs=f32(2, 2, 2, 8, CZ), zh=f32(2, 2, 2, 8, CZ),
-        fze=f32(2, 8, CZ), wyf=f32(2, 16, CZ), rows_y=f32(2, 16, CZ),
+        fze=f32(2, 8, CZ), wyf=f32(2, 16, CZ), rows_y=f32(2, 16, CZ), zp=f32(2, 8, CZ), gzp=f32(2, 8, CZ), hz=f32(2, 8, CZ),
         xs=pltpu.VMEM((AGG, 8 * CZ), BF16), ys=pltpu.VMEM((2 * AGG, 8 * CZ), BF16),
         acc=f32(AGG, 2 * AGG), mf=f32(7 * AGG, AGG), mm=pltpu.VMEM((7 * AGG, 2 * AGG), BF16),
         cs=f32(2, 8, CZ), ch=f32(2, 6, 8, CZ),

time: 63.5 us -> 62 us (0.976)
  Pallas kernels: 61.6 us -> 60.1 us
    pallas_call x1, Pallas kernels: 61.6 us -> 60.1 us  [body(): pl.pallas_call(kernel, out_shape=jax.ShapeDtypeStruct(field, F32), in_spe...]
where the time goes in v2:
time: 62 us; the launch traced here: 61.8 us
  Pallas kernels  60.1 us (97%)
  local copies, waits for them, and re-layouts  1.77 us (3%)
    pallas_call x1, Pallas kernels, body(): pl.pallas_call(kernel, out_shape=jax.ShapeDtypeStruct(field, F32), in_spe...  60.1 us
    unnamed x1, local copies, waits for them, and re-layouts  1.77 us

profile of v2, /device:TPU:1, one launch (start us, length us, event | category | flops | bytes accessed | tf_op | source)
XLA Modules:
  0.0 61.8 jit_solution(5093649712506786247)
XLA Ops:
  0.0 60.1 %shard_map.46 = f32[24,32,128]{2,1,0:T(8,128)} custom-call(f32[24,32,128]{2,1,0:T(8,128)} %b_hbm.1, f32[24,32,128]{2,1,0:T(8,128)} %k_hbm.1, f32[24,32,128]{2,1,0:T(8,128)} %a_hbm.1, s32[12,16,64]{2,1,0:T(8,128)} %l_hbm.1), custom_call_target="tpu_custom_call" | custom-call | tf_op jit(solution)/shard_map/pallas_call | solution.py:666
  60.1 1.8 %copy.6 = f32[24,32,128]{2,1,0:T(8,128)} copy(f32[24,32,128]{2,1,0:T(8,128)} %shard_map.46) | data formatting | bytes 786432

commit v3 on v2

--- a/solution.py
+++ b/solution.py
@@ -70,7 +70,7 @@
     b_hbm, k_hbm, a_hbm, l_hbm, out_hbm,
     bv, av, kp, lv, v, gw, c0, dg, sc, fx, fy, fz, gz, gy, gx, lc, el, ew,
     kxh, kyh, kzs, kzh, lxh, lys, lyh, lzs, lzh, xh, yh, zs, zh,
-    fze, wyf, rows_y, zp, gzp, hz, xs, ys, acc, mf, mm, cs, ch,
+    fze, wyf, rows_y, zp, gzp, hz, tp, xs, ys, acc, mf, mm, cs, ch,
     local_sem, send_sem, recv_sem,
 ):
     pos = [lax.axis_index(a) for a in AXES]
@@ -338,42 +338,64 @@
 
     lax.fori_loop(0, OWN_1, own_step, 0)
     load_b.wait()
+    own_d = []
+    own_b = []
+    for half in range(2):
+        packed_d = zero_tile
+        packed_b = zero_tile
+        for local in range(12):
+            packed_d = pack_plane(packed_d, dg[12 * half + local], local)
+            packed_b = pack_plane(packed_b, bv[12 * half + local], local)
+        own_d.append(packed_d)
+        own_b.append(packed_b)
     finish("k")
 
     gx[0] = harmonic(kp[1, cells], kxh[0])
     gx[1] = harmonic(kp[CX, cells], kxh[1])
     for half in range(2):
-        fze[half] = safe_harmonic(own_k[half], joined(kzh, half))
-
-    def first_step(half, carry):
-        packed = zero_tile
-        face_z = fze[half]
+        face_z = safe_harmonic(own_k[half], joined(kzh, half))
+        fze[half] = face_z
+        diag = own_d[half] + face_z
         for local in range(12):
             x = 12 * half + local
-            wall = unpack_plane(face_z, local)
-            wall = jnp.concatenate([jnp.where(rim, w, 0.0) for w in wall], axis=0)
-            gz[x] = wall
             low = harmonic(kp[x + 1, TOP : TOP + 8], kyh[0, x])
             high = harmonic(kp[x + 1, END - 8 : END], kyh[1, x])
             gy[0, x] = low
             gy[1, x] = high
-            diag = dg[x] + wall + jnp.concatenate([low, jnp.zeros((16, CZ), F32), high], axis=0)
-            if local == 0:
-                diag = diag + jnp.where(half == 0, gx[0], 0.0)
-            if local == 11:
-                diag = diag + jnp.where(half == 1, gx[1], 0.0)
-            scale = OMEGA_FINE / diag
-            first = scale * bv[x]
-            dg[x] = diag
-            sc[x] = scale
-            c0[x] = first
-            v[0, x + 1, cells] = first
-            packed = pack_plane(packed, first, local)
-        store_packed(zs.at[0], half, packed)
-        return carry
-
-    lax.fori_loop(0, 2, first_step, 0)
-    start("v", 0)
+            diag = diag + lane_roll(jnp.where(rim, low, 0.0), 8 * local)
+            diag = diag + lane_roll(jnp.where(rim, high, 0.0), 8 * local + 6)
+        diag = pack_plane(diag, gx[half], 11 * half)
+        first = OMEGA_FINE * own_b[half] / jnp.where(diag > 0.0, diag, 1.0)
+        store_packed(zs.at[0], half, first)
+    start("v", 0, (4, 5))
+
+    def first_part(x, g):
+        at = slice(8 * g, 8 * g + 8)
+        wall = jnp.where(rim, lane_roll(fze[x // 12], -2 * (4 * (x % 12) + g)), 0.0)
+        gz[x, at] = wall
+        diag = dg[x, at] + wall
+        if g == 0:
+            diag = diag + gy[0, x]
+        if g == 3:
+            diag = diag + gy[1, x]
+        if x == 0:
+            diag = diag + gx[0, at]
+        if x == CX - 1:
+            diag = diag + gx[1, at]
+        scale = OMEGA_FINE / diag
+        first = scale * bv[x, at]
+        dg[x, at] = diag
+        sc[x, at] = scale
+        c0[x, at] = first
+        v[0, x + 1, TOP + 8 * g : TOP + 8 * g + 8] = first
+
+    for x in range(CX):
+        for g in (range(4) if x in (0, CX - 1) else (0, 3)):
+            first_part(x, g)
+    start("v", 0, (2, 3, 0, 1))
+    for x in range(1, CX - 1):
+        for g in (1, 2):
+            first_part(x, g)
 
     def face_rows(block, carry):
         x = 2 * block
@@ -414,7 +436,7 @@
 
     lax.fori_loop(0, 2, pack_scale, 0)
 
-    def inner(slot, other):
+    def inner(slot):
         def step(half, carry):
             packed = zero_tile
             for local in range(12):
@@ -425,7 +447,7 @@
                 total = total + gw[2, x] * v[slot, x + 1, TOP - 1 : END - 1]
                 total = total + gw[3, x] * v[slot, x + 1, TOP + 1 : END + 1]
                 total = total + gw[4, x] * lane_roll(centre, 1) + gw[5, x] * lane_roll(centre, -1)
-                v[other, x + 1, cells] = total
+                tp[x] = total
                 packed = pack_plane(packed, total, local)
             zp[half] = packed
             return carry
@@ -448,32 +470,39 @@
                 packed = pack_plane(packed, gx[1] * xh[slot, 1], 11)
             store_packed(zs.at[other], half, packed)
 
-    def outer_rest(slot, other):
-        v[other, 1, cells] += gx[0] * xh[slot, 0]
-        v[other, CX, cells] += gx[1] * xh[slot, 1]
-
-        def step(half, carry):
-            halo_z = hz[half]
-            for local in range(12):
-                x = 12 * half + local
-                wall = jnp.concatenate(unpack_plane(halo_z, local), axis=0)
-                low = gy[0, x] * yh[slot, 0, x]
-                high = gy[1, x] * yh[slot, 1, x]
-                new = v[other, x + 1, cells] + gz[x] * wall
-                new = new + jnp.concatenate([low, jnp.zeros((16, CZ), F32), high], axis=0)
-                v[other, x + 1, cells] = new
-            return carry
-
-        lax.fori_loop(0, 2, step, 0)
-
-    inner(0, 1)
+    def finished(slot, x, g):
+        at = slice(8 * g, 8 * g + 8)
+        wall = lane_roll(hz[x // 12], -2 * (4 * (x % 12) + g))
+        new = tp[x, at] + gz[x, at] * wall
+        if g == 0:
+            new = new + gy[0, x] * yh[slot, 0, x]
+        if g == 3:
+            new = new + gy[1, x] * yh[slot, 1, x]
+        if x == 0:
+            new = new + gx[0, at] * xh[slot, 0, at]
+        if x == CX - 1:
+            new = new + gx[1, at] * xh[slot, 1, at]
+        return new
+
+    def outer_edges(slot, other):
+        for x in range(CX):
+            for g in (range(4) if x in (0, CX - 1) else (0, 3)):
+                v[other, x + 1, TOP + 8 * g : TOP + 8 * g + 8] = finished(slot, x, g)
+
+    def outer_middle(other):
+        for x in range(1, CX - 1):
+            for g in (1, 2):
+                v[other, x + 1, TOP + 8 * g : TOP + 8 * g + 8] = finished(None, x, g)
+
+    inner(0)
     lax.fori_loop(OWN_1, OWN_2, own_step, 0)
 
     finish("v", 0)
     outer_faces(0, 1)
     start("v", 1, (4, 5))
-    outer_rest(0, 1)
+    outer_edges(0, 1)
     start("v", 1, (2, 3, 0, 1))
+    outer_middle(1)
 
     lax.fori_loop(OWN_2, BX, own_step, 0)
     sum_own = acc[:, :AGG] + acc[:, AGG:]
@@ -524,14 +553,14 @@
         mm[AGG * t : AGG * (t + 1), :AGG] = high.astype(BF16)
         mm[AGG * t : AGG * (t + 1), AGG:] = low.astype(BF16)
 
-    inner(1, 0)
+    inner(1)
 
     def residual_step(turn, carry):
         for local in range(4):
             block = 4 * turn + local
             total = zero_plane
             for x in (2 * block, 2 * block + 1):
-                total = total + dg[x] * (v[0, x + 1, cells] - v[1, x + 1, cells])
+                total = total + dg[x] * (tp[x] - v[1, x + 1, cells])
             ew[0, block] = squeeze_cells(quad_sum(total * (1.0 / OMEGA_FINE)))
         return carry
 
@@ -617,7 +646,7 @@
         def _():
             finish_send("v", 1 - slot)
 
-        inner(slot, 1 - slot)
+        inner(slot)
         finish_recv("v", slot)
         outer_faces(slot, 1 - slot)
 
@@ -625,11 +654,13 @@
         def _():
             start("v", 1 - slot, (4, 5))
 
-        outer_rest(slot, 1 - slot)
+        outer_edges(slot, 1 - slot)
 
         @pl.when(turn < POST - 1)
         def _():
             start("v", 1 - slot, (2, 3, 0, 1))
+
+        outer_middle(1 - slot)
 
         return carry
 
@@ -658,7 +689,7 @@
         kxh=f32(2, CY, CZ), kyh=f32(2, CX, 8, CZ), kzs=f32(2, 2, 8, CZ), kzh=f32(2, 2, 8, CZ),
         lxh=f32(2, CY, CZ), lys=f32(2, 16, CZ), lyh=f32(2, 16, CZ), lzs=f32(2, 2, 8, CZ), lzh=f32(2, 2, 8, CZ),
         xh=f32(2, 2, CY, CZ), yh=f32(2, 2, CX, 8, CZ), zs=f32(2, 2, 2, 8, CZ), zh=f32(2, 2, 2, 8, CZ),
-        fze=f32(2, 8, CZ), wyf=f32(2, 16, CZ), rows_y=f32(2, 16, CZ), zp=f32(2, 8, CZ), gzp=f32(2, 8, CZ), hz=f32(2, 8, CZ),
+        fze=f32(2, 8, CZ), wyf=f32(2, 16, CZ), rows_y=f32(2, 16, CZ), zp=f32(2, 8, CZ), gzp=f32(2, 8, CZ), hz=f32(2, 8, CZ), tp=f32(*field),
         xs=pltpu.VMEM((AGG, 8 * CZ), BF16), ys=pltpu.VMEM((2 * AGG, 8 * CZ), BF16),
         acc=f32(AGG, 2 * AGG), mf=f32(7 * AGG, AGG), mm=pltpu.VMEM((7 * AGG, 2 * AGG), BF16),
         cs=f32(2, 8, CZ), ch=f32(2, 6, 8, CZ),

time: 62 us -> 61.7 us (level)
  no operation moved by 1% of the time
where the time goes in v3:
time: 61.7 us; the launch traced here: 61.5 us
  Pallas kernels  59.8 us (97%)
  local copies, waits for them, and re-layouts  1.77 us (3%)
    pallas_call x1, Pallas kernels, body(): pl.pallas_call(kernel, out_shape=jax.ShapeDtypeStruct(field, F32), in_spe...  59.8 us
    unnamed x1, local copies, waits for them, and re-layouts  1.77 us

profile of v3, /device:TPU:1, one launch (start us, length us, event | category | flops | bytes accessed | tf_op | source)
XLA Modules:
  0.0 61.5 jit_solution(4047353528314837479)
XLA Ops:
  0.0 59.8 %shard_map.46 = f32[24,32,128]{2,1,0:T(8,128)} custom-call(f32[24,32,128]{2,1,0:T(8,128)} %b_hbm.1, f32[24,32,128]{2,1,0:T(8,128)} %k_hbm.1, f32[24,32,128]{2,1,0:T(8,128)} %a_hbm.1, s32[12,16,64]{2,1,0:T(8,128)} %l_hbm.1), custom_call_target="tpu_custom_call" | custom-call | tf_op jit(solution)/shard_map/pallas_call | solution.py:697
  59.8 1.8 %copy.6 = f32[24,32,128]{2,1,0:T(8,128)} copy(f32[24,32,128]{2,1,0:T(8,128)} %shard_map.46) | data formatting | bytes 786432

commit v4 on v3

--- a/solution.py
+++ b/solution.py
@@ -12,7 +12,7 @@
 OMEGA_COARSE = 0.7
 CX, CY, CZ = 24, 32, 128
 BX = CX // 2
-OWN_1, OWN_2 = 4, 8
+OWN_1, OWN_2 = 2, 6
 TOP = 8
 END = TOP + CY
 AXES = ("gx", "gy", "gz")
@@ -267,7 +267,8 @@
         dg[x] = av[x] + fx_low + fx_high + fy_low + fy_high + fz_low + fz_high
         return fx_high, fy_high, fz_high
 
-    def block_step(block, fx_low):
+    def block_step(block, carry):
+        fx_low, cut_below = carry
         x = 2 * block
         fx_mid, fy_high_0, fz_high_0 = faces(x, fx_low)
         fx_high, fy_high_1, fz_high_1 = faces(x + 1, fx_mid)
@@ -276,7 +277,7 @@
         wy = row_roll(wy + lane_roll(wy, -1), -1)
         wz = fz_high_0 + fz_high_1
         wz = lane_roll(wz + row_roll(wz, -1), -1)
-        wa = 0.5 * quad_sum(av[x] + av[x + 1])
+        wa = quad_sum(av[x] + av[x + 1])
         own = lc[block, cells]
         lx = lc[jnp.minimum(block + 1, BX - 1), cells]
         ly = lc[block, TOP + 2 : END + 2]
@@ -284,6 +285,11 @@
         lx = jnp.where(lx == own, -1.0, lx)
         ly = jnp.where((ly == own) | (row >= CY - 2), -1.0, ly)
         lz = jnp.where((lz == own) | (lane >= CZ - 2), -1.0, lz)
+        cut_x = jnp.where(lx < 0.0, 0.0, wx)
+        cut_y = jnp.where(ly < 0.0, 0.0, wy)
+        cut_z = jnp.where(lz < 0.0, 0.0, wz)
+        leaving = wa + cut_below + cut_x + cut_y + row_roll(cut_y, 2) + cut_z + lane_roll(cut_z, 2)
+        ew[0, block] = squeeze_cells(leaving)
         same = ly == lx
         wx = wx + jnp.where(same, wy, 0.0)
         ly = jnp.where(same, -1.0, ly)
@@ -295,14 +301,14 @@
         lz = jnp.where(same, -1.0, lz)
         for n, field in enumerate((own, lx, ly, lz)):
             el[n, block] = squeeze_cells(field)
-        for n, field in enumerate((wa, wx, wy, wz)):
-            ew[n, block] = squeeze_cells(field)
-        return fx_high
-
-    def block_pair(turn, fx_low):
-        return block_step(2 * turn + 1, block_step(2 * turn, fx_low))
-
-    lax.fori_loop(0, BX // 2, block_pair, zero_plane)
+        for n, field in enumerate((wx, wy, wz)):
+            ew[n + 1, block] = squeeze_cells(field)
+        return fx_high, cut_x
+
+    def block_pair(turn, carry):
+        return block_step(2 * turn + 1, block_step(2 * turn, carry))
+
+    lax.fori_loop(0, BX // 2, block_pair, (zero_plane, zero_plane))
 
     number = rows_of((16, CZ)).astype(F32)
     numbers = [(number + 16.0 * q).astype(BF16) for q in range(8)]
@@ -331,8 +337,8 @@
     def own_step(block, carry):
         for m in range(8):
             at = slice(4 * m, 4 * m + 1)
-            pairs = [(el[n, block, at], ew[n, block, at]) for n in range(4)]
-            place(m * CZ, pairs[0][0], pairs)
+            pairs = [(el[n, block, at], ew[n, block, at]) for n in range(1, 4)]
+            place(m * CZ, el[0, block, at], pairs)
         acc[...] += lax.dot_general(xs[...], ys[...], NT, preferred_element_type=F32)
         return carry
 
@@ -494,7 +500,26 @@
             for g in (1, 2):
                 v[other, x + 1, TOP + 8 * g : TOP + 8 * g + 8] = finished(None, x, g)
 
+    wanted = rows_of((AGG, CZ)).astype(F32)
+
+    def gather_row(sums, label, value):
+        label = jnp.broadcast_to(label, (AGG, CZ))
+        return sums + jnp.where(label == wanted, jnp.broadcast_to(value, (AGG, CZ)), 0.0)
+
+    def restrict_step(block, sums):
+        for m in range(8):
+            at = slice(4 * m, 4 * m + 1)
+            sums = gather_row(sums, el[0, block, at], ew[0, block, at])
+        return sums
+
+    def aggregate_row(sums):
+        high, low = split(sums)
+        ones = jnp.ones((16, CZ), BF16)
+        out = lax.dot_general(ones, high.astype(BF16), NT, preferred_element_type=F32)
+        return (out + lax.dot_general(ones, low.astype(BF16), NT, preferred_element_type=F32))[0:8]
+
     inner(0)
+    diag_sums = lax.fori_loop(0, BX, restrict_step, jnp.zeros((AGG, CZ), F32))
     lax.fori_loop(OWN_1, OWN_2, own_step, 0)
 
     finish("v", 0)
@@ -504,9 +529,6 @@
     start("v", 1, (2, 3, 0, 1))
     outer_middle(1)
 
-    lax.fori_loop(OWN_2, BX, own_step, 0)
-    sum_own = acc[:, :AGG] + acc[:, AGG:]
-    mf[0:AGG] = sum_own + sum_own.T
     finish("l")
 
     def pair_rows(values):
@@ -539,19 +561,19 @@
             place(n * CZ, peer[at], [(own[at], weight[at])])
         depth = len(at_rows) * CZ
         tile = lax.dot_general(xs[:, :depth], ys[:, :depth], NT, preferred_element_type=F32)
-        mf[AGG * (d + 1) : AGG * (d + 2)] = tile[:, :AGG] + tile[:, AGG:]
-
-    column = zero_tile
-    for r in range(0, 7 * AGG, 8):
-        column = column + mf[r : r + 8]
-    coarse_diag = jnp.sum(column, axis=0, keepdims=True)
-    coarse_scale = OMEGA_COARSE / coarse_diag
-    square = (AGG, AGG)
-    mf[0:AGG] = jnp.where(rows_of(square) == lanes_of(square), 0.0, mf[0:AGG])
-    for t in range(7):
-        high, low = split(mf[AGG * t : AGG * (t + 1)] * coarse_scale)
+        mf[AGG * d : AGG * (d + 1)] = tile[:, :AGG] + tile[:, AGG:]
+        for r in at_rows:
+            diag_sums = gather_row(diag_sums, own[r : r + 1], weight[r : r + 1])
+
+    coarse_scale = OMEGA_COARSE / aggregate_row(diag_sums)
+
+    def store_tile(t, tile):
+        high, low = split(tile * coarse_scale[0:1])
         mm[AGG * t : AGG * (t + 1), :AGG] = high.astype(BF16)
         mm[AGG * t : AGG * (t + 1), AGG:] = low.astype(BF16)
+
+    for d in range(6):
+        store_tile(d + 1, mf[AGG * d : AGG * (d + 1)])
 
     inner(1)
 
@@ -565,18 +587,6 @@
         return carry
 
     lax.fori_loop(0, BX // 4, residual_step, 0)
-    wanted = rows_of((AGG, CZ)).astype(F32)
-
-    def gather_row(sums, label, value):
-        label = jnp.broadcast_to(label, (AGG, CZ))
-        return sums + jnp.where(label == wanted, jnp.broadcast_to(value, (AGG, CZ)), 0.0)
-
-    def restrict_step(block, sums):
-        for m in range(8):
-            at = slice(4 * m, 4 * m + 1)
-            sums = gather_row(sums, el[0, block, at], ew[0, block, at])
-        return sums
-
     sums = lax.fori_loop(0, BX, restrict_step, jnp.zeros((AGG, CZ), F32))
 
     finish("v", 1)
@@ -594,11 +604,7 @@
         for (d, peer, own, weight, at_rows), value in zip(faces_of[3 * side : 3 * side + 3], values):
             for r in at_rows:
                 sums = gather_row(sums, own[r : r + 1], value[r : r + 1])
-    high, low = split(sums)
-    ones = jnp.ones((16, CZ), BF16)
-    coarse_rhs = lax.dot_general(ones, high.astype(BF16), NT, preferred_element_type=F32)
-    coarse_rhs = coarse_rhs + lax.dot_general(ones, low.astype(BF16), NT, preferred_element_type=F32)
-    first_correction = coarse_scale * coarse_rhs[0:8]
+    first_correction = coarse_scale * aggregate_row(sums)
 
     def halves(values):
         high, low = split(values)
@@ -608,10 +614,14 @@
         values = values[:, :AGG] + values[:, AGG:]
         return values[0:8] + values[8:16]
 
-    def coarse_step(turn, correction):
-        slot = lax.rem(turn, 2)
+    def coarse_step(turn, correction, first=False):
+        slot = 0 if first else lax.rem(turn, 2)
         cs[slot] = correction
         start("c", slot)
+        if first:
+            lax.fori_loop(OWN_2, BX, own_step, 0)
+            sum_own = acc[:, :AGG] + acc[:, AGG:]
+            store_tile(0, sum_own + sum_own.T)
         image = jnp.dot(halves(correction), mm[0:AGG], preferred_element_type=F32)
         base = (1.0 - OMEGA_COARSE) * correction + first_correction
         base = base + both(image)
@@ -619,7 +629,7 @@
         beside = jnp.concatenate([ch[slot, d] for d in range(6)], axis=1)
         return base + both(jnp.dot(halves(beside), mm[AGG:], preferred_element_type=F32))
 
-    correction = lax.fori_loop(0, KC - 1, coarse_step, first_correction)
+    correction = lax.fori_loop(1, KC - 1, coarse_step, coarse_step(0, first_correction, True))
 
     def lift_step(half, carry):
         packed = zero_tile
@@ -691,7 +701,7 @@
         xh=f32(2, 2, CY, CZ), yh=f32(2, 2, CX, 8, CZ), zs=f32(2, 2, 2, 8, CZ), zh=f32(2, 2, 2, 8, CZ),
         fze=f32(2, 8, CZ), wyf=f32(2, 16, CZ), rows_y=f32(2, 16, CZ), zp=f32(2, 8, CZ), gzp=f32(2, 8, CZ), hz=f32(2, 8, CZ), tp=f32(*field),
         xs=pltpu.VMEM((AGG, 8 * CZ), BF16), ys=pltpu.VMEM((2 * AGG, 8 * CZ), BF16),
-        acc=f32(AGG, 2 * AGG), mf=f32(7 * AGG, AGG), mm=pltpu.VMEM((7 * AGG, 2 * AGG), BF16),
+        acc=f32(AGG, 2 * AGG), mf=f32(6 * AGG, AGG), mm=pltpu.VMEM((7 * AGG, 2 * AGG), BF16),
         cs=f32(2, 8, CZ), ch=f32(2, 6, 8, CZ),
     )
     return pl.pallas_call(

time: 61.7 us -> 59.4 us (0.963)
  Pallas kernels: 59.8 us -> 57.5 us
    pallas_call x1, Pallas kernels: 59.8 us -> 57.5 us  [body(): pl.pallas_call(kernel, out_shape=jax.ShapeDtypeStruct(field, F32), in_spe...]
where the time goes in v4:
time: 59.4 us; the launch traced here: 59.3 us
  Pallas kernels  57.5 us (97%)
  local copies, waits for them, and re-layouts  1.77 us (3%)
    pallas_call x1, Pallas kernels, body(): pl.pallas_call(kernel, out_shape=jax.ShapeDtypeStruct(field, F32), in_spe...  57.5 us
    unnamed x1, local copies, waits for them, and re-layouts  1.77 us

profile of v4, /device:TPU:1, one launch (start us, length us, event | category | flops | bytes accessed | tf_op | source)
XLA Modules:
  0.0 59.3 jit_solution(6020485510731962507)
XLA Ops:
  0.0 57.5 %shard_map.46 = f32[24,32,128]{2,1,0:T(8,128)} custom-call(f32[24,32,128]{2,1,0:T(8,128)} %b_hbm.1, f32[24,32,128]{2,1,0:T(8,128)} %k_hbm.1, f32[24,32,128]{2,1,0:T(8,128)} %a_hbm.1, s32[12,16,64]{2,1,0:T(8,128)} %l_hbm.1), custom_call_target="tpu_custom_call" | custom-call | tf_op jit(solution)/shard_map/pallas_call | solution.py:707
  57.5 1.8 %copy.6 = f32[24,32,128]{2,1,0:T(8,128)} copy(f32[24,32,128]{2,1,0:T(8,128)} %shard_map.46) | data formatting | bytes 786432

commit v5 on v4

--- a/solution.py
+++ b/solution.py
@@ -12,7 +12,7 @@
 OMEGA_COARSE = 0.7
 CX, CY, CZ = 24, 32, 128
 BX = CX // 2
-OWN_1, OWN_2 = 2, 6
+OWN_1, OWN_2 = 1, 5
 TOP = 8
 END = TOP + CY
 AXES = ("gx", "gy", "gz")
@@ -67,7 +67,7 @@
 
 
 def kernel(
-    b_hbm, k_hbm, a_hbm, l_hbm, out_hbm,
+    b_hbm, k_hbm, a_hbm, l_hbm, out,
     bv, av, kp, lv, v, gw, c0, dg, sc, fx, fy, fz, gz, gy, gx, lc, el, ew,
     kxh, kyh, kzs, kzh, lxh, lys, lyh, lzs, lzh, xh, yh, zs, zh,
     fze, wyf, rows_y, zp, gzp, hz, tp, xs, ys, acc, mf, mm, cs, ch,
@@ -279,7 +279,7 @@
         wz = lane_roll(wz + row_roll(wz, -1), -1)
         wa = quad_sum(av[x] + av[x + 1])
         own = lc[block, cells]
-        lx = lc[jnp.minimum(block + 1, BX - 1), cells]
+        lx = lc[min(block + 1, BX - 1), cells]
         ly = lc[block, TOP + 2 : END + 2]
         lz = lane_roll(own, -2)
         lx = jnp.where(lx == own, -1.0, lx)
@@ -305,10 +305,9 @@
             ew[n + 1, block] = squeeze_cells(field)
         return fx_high, cut_x
 
-    def block_pair(turn, carry):
-        return block_step(2 * turn + 1, block_step(2 * turn, carry))
-
-    lax.fori_loop(0, BX // 2, block_pair, (zero_plane, zero_plane))
+    below = (zero_plane, zero_plane)
+    for block in range(BX):
+        below = block_step(block, below)
 
     number = rows_of((16, CZ)).astype(F32)
     numbers = [(number + 16.0 * q).astype(BF16) for q in range(8)]
@@ -615,7 +614,7 @@
         return values[0:8] + values[8:16]
 
     def coarse_step(turn, correction, first=False):
-        slot = 0 if first else lax.rem(turn, 2)
+        slot = turn % 2
         cs[slot] = correction
         start("c", slot)
         if first:
@@ -629,7 +628,9 @@
         beside = jnp.concatenate([ch[slot, d] for d in range(6)], axis=1)
         return base + both(jnp.dot(halves(beside), mm[AGG:], preferred_element_type=F32))
 
-    correction = lax.fori_loop(1, KC - 1, coarse_step, coarse_step(0, first_correction, True))
+    correction = coarse_step(0, first_correction, True)
+    for turn in range(1, KC - 1):
+        correction = coarse_step(turn, correction)
 
     def lift_step(half, carry):
         packed = zero_tile
@@ -649,37 +650,25 @@
 
     lax.fori_loop(0, 2, lift_step, 0)
 
-    def post_step(turn, carry):
-        slot = 1 - lax.rem(turn, 2)
-
-        @pl.when(turn > 0)
-        def _():
+    start("v", 1)
+    for turn in range(POST):
+        slot = 1 - turn % 2
+        if turn:
             finish_send("v", 1 - slot)
-
         inner(slot)
         finish_recv("v", slot)
-        outer_faces(slot, 1 - slot)
-
-        @pl.when(turn < POST - 1)
-        def _():
+        if turn < POST - 1:
+            outer_faces(slot, 1 - slot)
             start("v", 1 - slot, (4, 5))
-
-        outer_edges(slot, 1 - slot)
-
-        @pl.when(turn < POST - 1)
-        def _():
+            outer_edges(slot, 1 - slot)
             start("v", 1 - slot, (2, 3, 0, 1))
-
-        outer_middle(1 - slot)
-
-        return carry
-
-    start("v", 1)
-    lax.fori_loop(0, POST, post_step, 0)
+            outer_middle(1 - slot)
     finish_send("v", 0)
-    store = pltpu.make_async_copy(v.at[1, 1 : CX + 1, cells], out_hbm, local_sem.at[0])
-    store.start()
-    store.wait()
+    for half in range(2):
+        hz[half] = joined(zh.at[0], half)
+    for x in range(CX):
+        for g in range(4):
+            out[x, 8 * g : 8 * g + 8] = finished(0, x, g)
 
 
 def body(right_side, conductance, absorption, block_agg):
@@ -706,9 +695,9 @@
     )
     return pl.pallas_call(
         kernel,
-        out_shape=jax.ShapeDtypeStruct(field, F32),
+        out_shape=pltpu.VMEM(field, F32),
         in_specs=[any_spec] * 4,
-        out_specs=any_spec,
+        out_specs=pl.BlockSpec(memory_space=pltpu.VMEM),
         scratch_shapes=list(scratch.values()) + [
             pltpu.SemaphoreType.DMA((4,)), pltpu.SemaphoreType.DMA((6, 6)), pltpu.SemaphoreType.DMA((6, 6)),
         ],

time: 59.4 us -> 58.4 us (0.983)
  local copies, waits for them, and re-layouts: 1.77 us -> 0.75 us
    unnamed x1, local copies, waits for them, and re-layouts: 1.77 us -> 0.75 us
where the time goes in v5:
time: 58.4 us; the launch traced here: 58.3 us
  Pallas kernels  57.5 us (98%)
  local copies, waits for them, and re-layouts  0.75 us (1%)
    pallas_call x1, Pallas kernels, body(): pl.pallas_call(kernel, out_shape=pltpu.VMEM(field, F32), in_specs=[any_sp...  57.5 us

profile of v5, /device:TPU:1, one launch (start us, length us, event | category | flops | bytes accessed | tf_op | source)
XLA Modules:
  0.0 58.3 jit_solution(10970000390921337409)
XLA Ops:
  0.0 57.5 %shard_map.46 = f32[24,32,128]{2,1,0:T(8,128)S(1)} custom-call(f32[24,32,128]{2,1,0:T(8,128)} %b_hbm.1, f32[24,32,128]{2,1,0:T(8,128)} %k_hbm.1, f32[24,32,128]{2,1,0:T(8,128)} %a_hbm.1, s32[12,16,64]{2,1,0:T(8,128)} %l_hbm.1), custom_call_target="tpu_custom_call" | custom-call | tf_op jit(solution)/shard_map/pallas_call | solution.py:696
  57.5 0.7 %copy.6 = f32[24,32,128]{2,1,0:T(8,128)} copy(f32[24,32,128]{2,1,0:T(8,128)S(1)} %shard_map.46) | data formatting | bytes 786432

commit v6 on v5

--- a/solution.py
+++ b/solution.py
@@ -101,8 +101,8 @@
                    zh.at[slot, 0], zh.at[slot, 1]]
             sem = 2 + slot
         else:
-            src = [cs.at[slot]] * 6
-            dst = [ch.at[slot, d] for d in range(6)]
+            src = [cs.at[slot, 0:1]] * 6
+            dst = [ch.at[slot, d, 0:1] for d in range(6)]
             sem = 4 + slot
         return src, dst, sem
 
@@ -625,7 +625,7 @@
         base = (1.0 - OMEGA_COARSE) * correction + first_correction
         base = base + both(image)
         finish("c", slot)
-        beside = jnp.concatenate([ch[slot, d] for d in range(6)], axis=1)
+        beside = jnp.concatenate([jnp.broadcast_to(ch[slot, d, 0:1], (8, CZ)) for d in range(6)], axis=1)
         return base + both(jnp.dot(halves(beside), mm[AGG:], preferred_element_type=F32))
 
     correction = coarse_step(0, first_correction, True)

time: 58.4 us -> 58.1 us (level)
  no operation moved by 1% of the time
where the time goes in v6:
time: 58.1 us; the launch traced here: 58 us
  Pallas kernels  57.3 us (99%)
  local copies, waits for them, and re-layouts  0.75 us (1%)
    pallas_call x1, Pallas kernels, body(): pl.pallas_call(kernel, out_shape=pltpu.VMEM(field, F32), in_specs=[any_sp...  57.3 us

profile of v6, /device:TPU:1, one launch (start us, length us, event | category | flops | bytes accessed | tf_op | source)
XLA Modules:
  0.0 58.0 jit_solution(4679392432791071103)
XLA Ops:
  0.0 57.3 %shard_map.46 = f32[24,32,128]{2,1,0:T(8,128)S(1)} custom-call(f32[24,32,128]{2,1,0:T(8,128)} %b_hbm.1, f32[24,32,128]{2,1,0:T(8,128)} %k_hbm.1, f32[24,32,128]{2,1,0:T(8,128)} %a_hbm.1, s32[12,16,64]{2,1,0:T(8,128)} %l_hbm.1), custom_call_target="tpu_custom_call" | custom-call | tf_op jit(solution)/shard_map/pallas_call | solution.py:696
  57.3 0.7 %copy.6 = f32[24,32,128]{2,1,0:T(8,128)} copy(f32[24,32,128]{2,1,0:T(8,128)S(1)} %shard_map.46) | data formatting | bytes 786432

commit v7 on v6

--- a/solution.py
+++ b/solution.py
@@ -518,7 +518,6 @@
         return (out + lax.dot_general(ones, low.astype(BF16), NT, preferred_element_type=F32))[0:8]
 
     inner(0)
-    diag_sums = lax.fori_loop(0, BX, restrict_step, jnp.zeros((AGG, CZ), F32))
     lax.fori_loop(OWN_1, OWN_2, own_step, 0)
 
     finish("v", 0)
@@ -528,6 +527,7 @@
     start("v", 1, (2, 3, 0, 1))
     outer_middle(1)
 
+    diag_sums = lax.fori_loop(0, BX, restrict_step, jnp.zeros((AGG, CZ), F32))
     finish("l")
 
     def pair_rows(values):

time: 58.1 us -> 58.4 us (level)
  no operation moved by 1% of the time
where the time goes in v7:
time: 58.4 us; the launch traced here: 58.3 us
  Pallas kernels  57.5 us (98%)
  local copies, waits for them, and re-layouts  0.75 us (1%)
    pallas_call x1, Pallas kernels, body(): pl.pallas_call(kernel, out_shape=pltpu.VMEM(field, F32), in_specs=[any_sp...  57.5 us

profile of v7, /device:TPU:1, one launch (start us, length us, event | category | flops | bytes accessed | tf_op | source)
XLA Modules:
  0.0 58.3 jit_solution(13133216784450388136)
XLA Ops:
  0.0 57.5 %shard_map.46 = f32[24,32,128]{2,1,0:T(8,128)S(1)} custom-call(f32[24,32,128]{2,1,0:T(8,128)} %b_hbm.1, f32[24,32,128]{2,1,0:T(8,128)} %k_hbm.1, f32[24,32,128]{2,1,0:T(8,128)} %a_hbm.1, s32[12,16,64]{2,1,0:T(8,128)} %l_hbm.1), custom_call_target="tpu_custom_call" | custom-call | tf_op jit(solution)/shard_map/pallas_call | solution.py:696
  57.5 0.7 %copy.6 = f32[24,32,128]{2,1,0:T(8,128)} copy(f32[24,32,128]{2,1,0:T(8,128)S(1)} %shard_map.46) | data formatting | bytes 786432
